TPU v7x, 32 devices: a whole 2x2x4 slice. The times are simulated.
32 devices in a mesh: wide: 4 (over x, core), narrow: 8 (over z, y).
Axes of the slice: x: 2, y: 2, z: 4, core: 2. Of those that a mesh axis runs over, the one named last changes fastest.
Arguments:
- grad_parts: bfloat16 [4, 3584, 8192], P('wide', 'narrow'), may hold values from -6 to 6
- master: bfloat16 [3584, 8192], P('narrow'), may hold values from -0.1875 to 0.1875
- moment_one: float32 [3584, 8192], P('narrow'), may hold values from -4 to 4
- moment_two: float32 [3584, 8192], P('narrow'), may hold values from 0.01 to 1
- gate_up: bfloat16 [3584, 2, 8192], P(None, None, 'narrow'), may hold values from -0.09375 to 0.09375
- tokens: bfloat16 [64, 3584], P(('wide', 'narrow')), may hold values from -6 to 6
- expert_ids: int32 [64, 4], P(('wide', 'narrow')), may hold values from 0 to 7, all different within a row; in each aligned block of 2 rows (0 to 1, 2 to 3, ...) at most 2 rows name the same one
- gate_vals: bfloat16 [64, 4], P(('wide', 'narrow')), may hold values from 0.049804688 to 1
Outputs:
- new_master: bfloat16 [3584, 8192], P('narrow')
- new_one: float32 [3584, 8192], P('narrow')
- new_two: float32 [3584, 8192], P('narrow')
- combined: bfloat16 [64, 3584], P(('wide', 'narrow'))
Inputs may be any that keep to these rules, and one draw needn't show every extreme that they name: `expert_ids`: each token names 4 distinct experts; each device's 2 tokens name every expert at most 2 times (which follows from the distinct ids), and some device names one expert twice.
All inputs are finite; a program needn't handle non-finite values.
Results may differ from a plain program's by a relative error of at most 0.022.
Values may be sent and summed in bfloat16 or wider, within the bound.
No kernel may reach another device: no remote copies, remote signals or barrier semaphores. Data moves between devices by JAX's collectives and lax.ppermute only.
A program may use at most 192 MiB of HBM per device.

v0:
```python
import functools

import jax
import jax.numpy as jnp
from jax import lax
from jax.experimental import pallas as pl
from jax.experimental.pallas import tpu as pltpu
from jax.sharding import PartitionSpec as P


EXPERTS = 8
QBLOCK = 128
LANES = 128
VMEM_GRANT = 58 << 20

beta_first = 0.9
beta_second = 0.95
learn_rate = 0.003
adam_eps = 1e-08
quant_limit = 448.0
amax_eps = 1e-06
bias_first = 1.0 - 0.9**10
bias_second = 1.0 - 0.95**10


def adam_kernel(far, block, down, aliased, base, *refs):
    refs = list(refs)
    terms = [refs.pop(0) for _ in range(far[0] + far[1])]
    state = [refs.pop(0) for _ in range(3)]
    if down:
        hidden, weight = refs.pop(0), refs.pop(0)
    refs = refs[4 if aliased else 0 :]
    fresh = [refs.pop(0) for _ in range(3)]
    comb = refs.pop(0) if down else None
    token = refs.pop(0)
    term_v = [refs.pop(0) for _ in terms]
    state_v = [refs.pop(0) for _ in range(3)]
    in_sem, out_sem = refs
    rows, cols = state_v[0].shape
    toks = comb.shape[1] if down else 0

    def copies(j):
        there = pl.ds(pl.multiple_of(base[0] + j * block, 8), block)
        here = pl.ds(pl.multiple_of(j * block, 8), block)
        pairs = [(t.at[there if q < far[0] else here], v) for q, (t, v) in enumerate(zip(terms, term_v))]
        pairs += [(s.at[there], v) for s, v in zip(state, state_v)]
        ins = [
            pltpu.make_async_copy(s, v.at[here], in_sem.at[q, j]) for q, (s, v) in enumerate(pairs)
        ]
        outs = [
            pltpu.make_async_copy(v.at[here], f.at[there], out_sem.at[q, j])
            for q, (v, f) in enumerate(zip(state_v, fresh))
        ]
        return ins, outs, here

    def begin(j, carry):
        for copy in copies(j)[0]:
            copy.start()
        return carry

    def adam(here, at):
        read = lambda ref: ref[here, at].astype(jnp.float32)
        grad = read(term_v[0])
        if far[0] == 2:
            grad = (grad + read(term_v[1])).astype(jnp.bfloat16).astype(jnp.float32)
        if len(term_v) > 1:
            grad = grad + read(term_v[-1])
        first = beta_first * read(state_v[1]) + (1.0 - beta_first) * grad
        second = beta_second * read(state_v[2]) + (1.0 - beta_second) * grad * grad
        state_v[1][here, at] = first
        state_v[2][here, at] = second
        spread = second * (1.0 / bias_second)
        step = first * (learn_rate / bias_first) / (spread * lax.rsqrt(spread) + adam_eps)
        updated = read(state_v[0]) - step
        state_v[0][here, at] = updated.astype(jnp.bfloat16)
        return updated

    def step_down(here):
        slices = weight.shape[0]
        unit = cols // slices
        lanes = hidden.shape[1]
        group = lanes // toks
        lane_block = lax.broadcasted_iota(jnp.int32, (block, lanes), 1) // toks
        total = jnp.zeros((block, lanes), jnp.float32)
        for s in range(slices):
            updated = adam(here, slice(s * unit, (s + 1) * unit))
            partial = jnp.zeros((block, lanes), jnp.float32)
            for g in range(0, unit // QBLOCK, group):
                scales = jnp.zeros((block, lanes), jnp.float32)
                pieces = []
                for b in range(group):
                    cells = updated[:, (g + b) * QBLOCK : (g + b + 1) * QBLOCK]
                    amax = jnp.max(jnp.abs(cells), axis=1, keepdims=True)
                    scale = (amax + amax_eps) * (1.0 / quant_limit)
                    scale = scale.astype(jnp.bfloat16).astype(jnp.float32)
                    scales = jnp.where(lane_block == b, scale, scales)
                    pieces.append((cells * (1.0 / scale)).astype(jnp.bfloat16))
                at = slice(s * unit + g * QBLOCK, s * unit + (g + group) * QBLOCK)
                dots = jnp.dot(
                    jnp.concatenate(pieces, axis=1) if group > 1 else pieces[0],
                    hidden[at, :],
                    preferred_element_type=jnp.float32,
                )
                partial = partial + dots * scales
            turn = toks
            while turn < lanes:
                partial = partial + pltpu.roll(partial, turn, 1)
                turn *= 2
            total = total + partial.astype(jnp.bfloat16).astype(jnp.float32) * weight[s : s + 1, :]
        comb[here, :] = total[:, :toks]

    def step_plain(here):
        width = 1024 if cols % 1024 == 0 else LANES

        def part(c, carry):
            adam(here, pl.ds(pl.multiple_of(c * width, LANES), width))
            return carry

        lax.fori_loop(0, cols // width, part, 0)

    def step(j, carry):
        ins, outs, here = copies(j)
        for copy in ins:
            copy.wait()
        (step_down if down else step_plain)(here)
        for copy in outs:
            copy.start()
        return carry

    def finish(j, carry):
        for copy in copies(j)[1]:
            copy.wait()
        return carry

    token[...] = jnp.zeros_like(token)
    for phase in (begin, step, finish):
        lax.fori_loop(0, rows // block, phase, 0)


def adam_rows(base, whole, local, state, outs, token, rows, block, hidden=None, weight=None, toks=0):
    full, cols = state[0].shape
    down = hidden is not None
    anywhere, vmem = pl.BlockSpec(memory_space=pltpu.HBM), pl.BlockSpec(memory_space=pltpu.VMEM)
    args = [*whole, *local, *state]
    in_specs = [anywhere] * len(whole) + [pl.BlockSpec(memory_space=pl.ANY)] * len(local)
    in_specs += [anywhere] * len(state)
    if down:
        args += [hidden, weight]
        in_specs += [vmem] * 2
    aliases = {}
    if outs is not None:
        aliases = {1 + len(args) + i: i for i in range(3)}
        in_specs += [anywhere] * 3 + [vmem]
        args += [*outs, token]
    terms = len(whole) + len(local)
    cells = rows * cols
    scratch = [pltpu.VMEM((rows, cols), jnp.bfloat16)] * (terms + 1)
    scratch += [pltpu.VMEM((rows, cols), jnp.float32)] * 2
    scratch += [
        pltpu.SemaphoreType.DMA((terms + 3, rows // block)),
        pltpu.SemaphoreType.DMA((3, rows // block)),
    ]
    result = pl.pallas_call(
        functools.partial(adam_kernel, (len(whole), len(local)), block, down, outs is not None),
        grid_spec=pltpu.PrefetchScalarGridSpec(
            num_scalar_prefetch=1,
            grid=(),
            in_specs=in_specs,
            out_specs=[anywhere] * 3 + [vmem] * (1 + down),
            scratch_shapes=scratch,
        ),
        out_shape=[
            jax.ShapeDtypeStruct((full, cols), jnp.bfloat16),
            jax.ShapeDtypeStruct((full, cols), jnp.float32),
            jax.ShapeDtypeStruct((full, cols), jnp.float32),
        ]
        + [jax.ShapeDtypeStruct((rows, toks), jnp.float32)] * down
        + [jax.ShapeDtypeStruct((8, LANES), jnp.float32)],
        input_output_aliases=aliases,
        compiler_params=pltpu.CompilerParams(vmem_limit_bytes=VMEM_GRANT),
        cost_estimate=pl.CostEstimate(
            flops=cells * (40 + 2 * toks),
            bytes_accessed=cells * (20 + 2 * terms),
            transcendentals=cells * 3,
        ),
    )(base.reshape(1), *args)
    return result[:3], result[-1], result[3]


def block_diagonal(hidden, toks):
    cells = hidden.shape[0]
    group = max(1, LANES // toks)
    which = (jnp.arange(cells) // QBLOCK % group)[:, None, None] == jnp.arange(group)[None, :, None]
    out = jnp.where(which, hidden[:, None, :], jnp.zeros((), hidden.dtype))
    return out.reshape(cells, group * toks), group


def token_weights(expert_ids, gate_vals):
    onehot = (expert_ids[:, :, None] == jnp.arange(EXPERTS, dtype=jnp.int32)).astype(jnp.float32)
    return jnp.sum(onehot * gate_vals.astype(jnp.float32)[:, :, None], axis=1).astype(jnp.bfloat16)


def up_project(rows, gate_up):
    proj = jnp.einsum("td,dgu->gtu", rows, gate_up, preferred_element_type=jnp.float32)
    return (jax.nn.silu(proj[0]) * proj[1]).astype(jnp.bfloat16)


def plain_body(grads, state, gate_up, tokens, expert_ids, gate_vals):
    narrow = lax.axis_size("narrow")
    tok_count, width = tokens.shape
    full = grads.shape[0]
    spread = lambda x: lax.all_to_all(
        jnp.broadcast_to(x[None], (narrow,) + x.shape), "narrow", 0, 0, tiled=True
    )
    total = lax.psum(grads, "wide")
    local = jnp.pad(token_weights(expert_ids, gate_vals), ((0, 0), (0, LANES - EXPERTS)))
    toks = narrow * tok_count
    every = spread(jnp.concatenate([tokens, local], axis=1)).reshape(toks, -1)
    hidden = spread(up_project(every[:, :width], gate_up))
    hidden = hidden.transpose(0, 2, 1).reshape(-1, toks)
    hidden, group = block_diagonal(hidden, toks)
    weight = jnp.repeat(every[:, width : width + EXPERTS].T, narrow // EXPERTS, axis=0)
    weight = jnp.tile(weight.astype(jnp.float32), (1, group))
    zero = jnp.zeros((), jnp.int32)
    outs, _, comb = adam_rows(zero, (total,), (), state, None, None, full, 8, hidden, weight, toks)
    out = comb.T.astype(jnp.bfloat16).reshape(narrow, tok_count, full)
    out = lax.all_to_all(out, "narrow", 0, 0, tiled=True)
    return (*outs, out.transpose(1, 0, 2).reshape(tok_count, narrow * full))


together = lax.optimization_barrier


def xor_gather(x, axes, size, groups, early=None, meet=None):
    index = lax.axis_index(axes)
    for turn, bits in enumerate(groups):
        if turn and meet is not None:
            x = meet(x)
        masks = [0]
        for bit in bits:
            masks += [m | bit for m in masks]
        got = [lax.ppermute(x, axes, [(i, i ^ m) for i in range(size)]) for m in masks[1:]]
        got = [x] + got
        if not turn and early is not None:
            got = early(got)
        x = jnp.stack(got).reshape((2,) * len(bits) + x.shape)
        for place, bit in enumerate(bits):
            axis = len(bits) - 1 - place
            x = jnp.where(index & bit, jnp.flip(x, axis), x)
    return x


def row_chunks(half):
    sizes, left = [], half
    for share in CHUNKS:
        take = min(left, max(8, half * share // sum(CHUNKS) // 16 * 16))
        sizes.append(take)
        left -= take
    sizes[0] += left
    return [n for n in sizes if n]


CHUNKS = (80, 48, 48, 32, 16)


def body(grad_parts, master, moment_one, moment_two, gate_up, tokens, expert_ids, gate_vals):
    grads = grad_parts[0]
    full, _ = grads.shape
    wide, narrow = lax.axis_size("wide"), lax.axis_size("narrow")
    state = (master, moment_one, moment_two)
    tok_count, width = tokens.shape
    if wide != 4 or narrow != 8 or full % 32:
        return plain_body(grads, state, gate_up, tokens, expert_ids, gate_vals)

    both = ("wide", "narrow")
    core = lax.axis_index("wide") & 1
    swap_core = lambda a: lax.ppermute(a, "wide", [(i, i ^ 1) for i in range(wide)])
    swap_chip = lambda a: lax.ppermute(a, "wide", [(i, i ^ 2) for i in range(wide)])
    half = full // 2
    sizes = row_chunks(half)
    starts = [sum(sizes[:k]) for k in range(len(sizes))]
    mine, theirs = core * half, (1 - core) * half
    rows_of = lambda a, at, n: lax.dynamic_slice_in_dim(a, at, n, 0)

    lead = swap_core(rows_of(grads, theirs, sizes[0]))
    held, lead = together((grads, lead))
    other = swap_core(held)
    sums = [rows_of(grads, mine, sizes[0]) + lead]
    sums += [
        rows_of(grads, mine + at, n) + rows_of(other, mine + at, n)
        for at, n in zip(starts[1:], sizes[1:])
    ]
    got = []

    def send(k):
        got.append(swap_chip(sums[k]))

    def send_first(x):
        x, sums[0] = together((x, sums[0]))
        send(0)
        return x

    def send_rest(x):
        x, *sums[1:] = together((x, *sums[1:]))
        for k in range(1, len(sums)):
            send(k)
        return x

    toks = 2 * narrow * tok_count
    every = xor_gather(tokens, both, wide * narrow, ((1, narrow), (2, 4)), send_first)
    every = every.transpose(2, 0, 1, 3, 4, 5).reshape(toks, width)
    piece = up_project(every, gate_up)
    local = jnp.pad(token_weights(expert_ids, gate_vals), ((0, 0), (0, LANES - EXPERTS)))
    local = xor_gather(local, "wide", wide, ((1,),)).reshape(2 * tok_count, LANES)
    local = jnp.pad(local, ((0, toks - 2 * tok_count), (0, 0)))
    piece = jnp.concatenate([piece, local], axis=1)
    hidden = xor_gather(piece, "narrow", narrow, ((1,), (2, 4)), None, send_rest)
    hidden = hidden.reshape(narrow, toks, -1)
    unit = gate_up.shape[2]
    weight = hidden[:, : 2 * tok_count, unit : unit + EXPERTS]
    weight = weight.reshape(narrow, 2, tok_count, EXPERTS).transpose(3, 1, 0, 2).reshape(EXPERTS, toks)
    hidden = hidden[:, :, :unit].transpose(0, 2, 1).reshape(-1, toks)
    hidden, group = block_diagonal(hidden, toks)
    weight = jnp.tile(jnp.repeat(weight.astype(jnp.float32), narrow // EXPERTS, axis=0), (1, group))

    outs, combs, token = None, [], None
    for k, (at, n) in enumerate(zip(starts, sizes)):
        if k:
            got[k], token = together((got[k], token))
        relay = swap_core(got[k])
        own = lambda outs, token: adam_rows(
            mine + at, (), (sums[k], got[k]), state, outs, token, n, 16, hidden, weight, toks
        )
        rest = lambda outs, token: adam_rows(theirs + at, (grads, other), (relay,), state, outs, token, n, 16)
        if k == 0:
            outs, token, _ = rest(outs, token)
        outs, token, comb = own(outs, token)
        combs.append(comb)
        if k:
            outs, token, _ = rest(outs, token)
    out = jnp.concatenate(combs, axis=0).T.astype(jnp.bfloat16).reshape(2 * narrow, tok_count, half)
    groups = [[(2 * x + c) * narrow + n for c in range(2) for n in range(narrow)] for x in range(wide // 2)]
    out = lax.all_to_all(out, both, 0, 0, axis_index_groups=groups, tiled=True)
    out = out.reshape(2, narrow, tok_count, half).transpose(2, 1, 0, 3).reshape(tok_count, narrow * full)
    return (*outs, out)


def solution(mesh):
    in_specs = (
        P("wide", "narrow", None),
        P("narrow", None),
        P("narrow", None),
        P("narrow", None),
        P(None, None, "narrow"),
        P(("wide", "narrow"), None),
        P(("wide", "narrow"), None),
        P(("wide", "narrow"), None),
    )
    out_specs = (
        P("narrow", None),
        P("narrow", None),
        P("narrow", None),
        P(("wide", "narrow"), None),
    )
    return jax.shard_map(body, mesh=mesh, in_specs=in_specs, out_specs=out_specs, check_vma=False)
```

profile of v0, /device:TPU:0, one launch (start us, length us, event | category | flops | bytes accessed | tf_op | source)
XLA Modules:
  0.0 155.7 jit_solution(2449965754186689602)
XLA Ops:
  0.6 1.4 dynamic-slice_bitcast_fusion
  2.6 2.6 %collective-permute-start.2 = (bf16[2,3584]{1,0:T(2,128)(2,1)}, bf16[2,3584]{1,0:T(2,128)(2,1)S(1)}, u32[]{:S(2)}, u32[]{:S(2)}) collective-permute-start(bf16[2,3584]{1,0:T(2,128)(2,1)} %param.13), channel_id=1, source_target_pairs={{0,1},{1,0},{2,3},{3,2},{4,5},{5,4},{6,7},{7,6},{8,9},{9,8},{10,11... | collective-permute-start | bytes 43016 | tf_op jit(solution)/shard_map/ppermute | solution.py:242
  5.4 0.7 convert_element_type.35
  6.0 0.8 select_reduce_fusion
  7.2 0.8 collective-permute-done.8
  8.1 1.6 %bitcast_add_fusion.refs_0_ = bf16[80,8192]{1,0:T(8,128)(2,1)S(1)} fusion(bf16[80,8192]{1,0:T(8,128)(2,1)S(1)} %collective-permute-done, bf16[1,448,8192]{2,1,0:T(8,128)(2,1)} %param.8, s32[]{:T(128)S(6)} %select_n.114), kind=kLoop, calls=%fused_computation.3 | loop fusion | flops 2621440 | bytes 3932164 | tf_op jit(solution)/shard_map/add | solution.py:288
  10.2 0.8 pad_maximum_fusion.3
  11.1 1.9 %collective-permute-start.5 = (bf16[2,2,2,3584]{3,2,1,0:T(2,128)(2,1)S(1)}, bf16[2,2,2,3584]{3,2,1,0:T(2,128)(2,1)S(1)}, u32[]{:S(2)}, u32[]{:S(2)}) collective-permute-start(bf16[2,2,2,3584]{3,2,1,0:T(2,128)(2,1)S(1)} %broadcast_select_fusion.4), channel_id=1, source_target_pairs={{0,2},{1,3},{2,0},{3,1},{4,6},{5,7},{6,4},{7,5},{8,10},{9,11},{10,... | collective-permute-start | bytes 172040 | tf_op jit(solution)/shard_map/ppermute | solution.py:242
  13.0 2.6 %collective-permute-start.6 = (bf16[2,2,2,3584]{3,2,1,0:T(2,128)(2,1)S(1)}, bf16[2,2,2,3584]{3,2,1,0:T(2,128)(2,1)S(1)}, u32[]{:S(2)}, u32[]{:S(2)}) collective-permute-start(bf16[2,2,2,3584]{3,2,1,0:T(2,128)(2,1)S(1)} %broadcast_select_fusion.4), channel_id=1, source_target_pairs={{0,4},{1,5},{2,6},{3,7},{4,0},{5,1},{6,2},{7,3},{8,12},{9,13},{10,... | collective-permute-start | bytes 172040 | tf_op jit(solution)/shard_map/ppermute | solution.py:242
  15.7 1.8 %collective-permute-start.14 = (bf16[80,8192]{1,0:T(8,128)(2,1)S(1)}, bf16[80,8192]{1,0:T(8,128)(2,1)}, u32[]{:S(2)}, u32[]{:S(2)}) collective-permute-start(bf16[80,8192]{1,0:T(8,128)(2,1)S(1)} %bitcast_add_fusion.refs_0_), channel_id=1, source_target_pairs={{0,16},{8,24},{16,0},{24,8},{1,17},{9,25},{17,1},{25,9},{2,18},{10... | collective-permute-start | bytes 3932168 | tf_op jit(solution)/shard_map/ppermute | solution.py:278
  17.4 2.1 %collective-permute-done.6 = bf16[2,2,2,3584]{3,2,1,0:T(2,128)(2,1)S(1)} collective-permute-done((bf16[2,2,2,3584]{3,2,1,0:T(2,128)(2,1)S(1)}, bf16[2,2,2,3584]{3,2,1,0:T(2,128)(2,1)S(1)}, u32[]{:S(2)}, u32[]{:S(2)}) %collective-permute-start.6) | collective-permute-done | bytes 57376 | tf_op jit(solution)/shard_map/ppermute | solution.py:242
  19.5 2.1 %collective-permute-done.7 = bf16[2,2,2,3584]{3,2,1,0:T(2,128)(2,1)S(1)} collective-permute-done((bf16[2,2,2,3584]{3,2,1,0:T(2,128)(2,1)S(1)}, bf16[2,2,2,3584]{3,2,1,0:T(2,128)(2,1)S(1)}, u32[]{:S(2)}, u32[]{:S(2)}) %collective-permute-start.7) | collective-permute-done | bytes 57376 | tf_op jit(solution)/shard_map/ppermute | solution.py:242
  22.6 9.5 %fusion.2 = f32[2,32,1024]{2,1,0:T(8,128)S(1)} fusion(bf16[32,3584,1]{1,0,2:T(8,128)(2,1)S(1)} %reshape.162, bf16[3584,2,1024]{2,1,0:T(2,128)(2,1)} %param.12), kind=kOutput, calls=%fused_computation.5 | convolution fusion | flops 469762048 | bytes 15171584 | tf_op jit(solution)/shard_map/td,dgu->gtu/dot_general | solution.py:204
  32.2 1.6 %collective-permute-start.9 = (bf16[32,1152]{1,0:T(8,128)(2,1)S(1)}, bf16[32,1152]{1,0:T(8,128)(2,1)S(1)}, u32[]{:S(2)}, u32[]{:S(2)}) collective-permute-start(bf16[32,1152]{1,0:T(8,128)(2,1)S(1)} %get-tuple-element.135), channel_id=1, source_target_pairs={{0,1},{1,0},{2,3},{3,2},{4,5},{5,4},{6,7},{7,6},{8,9},{9,8},{10,11... | collective-permute-start | bytes 221192 | tf_op jit(solution)/shard_map/ppermute | solution.py:242
  33.8 2.8 %collective-permute-done.9 = bf16[32,1152]{1,0:T(8,128)(2,1)S(1)} collective-permute-done((bf16[32,1152]{1,0:T(8,128)(2,1)S(1)}, bf16[32,1152]{1,0:T(8,128)(2,1)S(1)}, u32[]{:S(2)}, u32[]{:S(2)}) %collective-permute-start.9) | collective-permute-done | bytes 73760 | tf_op jit(solution)/shard_map/ppermute | solution.py:242
  36.7 9.6 %collective-permute-done.14.refs_1_ = bf16[80,8192]{1,0:T(8,128)(2,1)} collective-permute-done((bf16[80,8192]{1,0:T(8,128)(2,1)S(1)}, bf16[80,8192]{1,0:T(8,128)(2,1)}, u32[]{:S(2)}, u32[]{:S(2)}) %collective-permute-start.14) | collective-permute-done | bytes 1310752 | tf_op jit(solution)/shard_map/ppermute | solution.py:278
  46.3 1.3 bitcast_add_fusion.3.refs_0_
  47.6 2.0 %bitcast_add_fusion.4.refs_0_ = bf16[16,8192]{1,0:T(8,128)(2,1)} fusion(bf16[448,8192]{1,0:T(8,128)(2,1)} %collective-permute-done.1.refs_1_, s32[]{:T(128)S(6)} %select_n.125, bf16[1,448,8192]{2,1,0:T(8,128)(2,1)} %param.8), kind=kLoop, calls=%fused_computation.14 | loop fusion | flops 524288 | bytes 786436 | tf_op jit(solution)/shard_map/add | solution.py:290
  49.6 3.1 %bitcast_add_fusion.1 = (bf16[48,8192]{1,0:T(8,128)(2,1)S(1)}, bf16[48,8192]{1,0:T(8,128)(2,1)}) fusion(bf16[448,8192]{1,0:T(8,128)(2,1)} %collective-permute-done.1.refs_1_, s32[]{:T(128)S(6)} %select_n.123, bf16[1,448,8192]{2,1,0:T(8,128)(2,1)} %param.8, s32[]{:T(128)S(6)} %select_n.122), kind=kLoop, calls=%fused_computation.8 | loop fusion | flops 3145728 | bytes 4718600 | tf_op jit(solution)/shard_map/add | solution.py:290
  52.7 0.6 collective-permute-start.15
  53.3 3.5 %collective-permute-start.16 = (bf16[2,32,1152]{2,1,0:T(8,128)(2,1)S(1)}, bf16[2,32,1152]{2,1,0:T(8,128)(2,1)S(1)}, u32[]{:S(2)}, u32[]{:S(2)}) collective-permute-start(bf16[2,32,1152]{2,1,0:T(8,128)(2,1)S(1)} %reverse_select_fusion.2), channel_id=1, source_target_pairs={{0,4},{1,5},{2,6},{3,7},{4,0},{5,1},{6,2},{7,3},{8,12},{9,13},{10,... | collective-permute-start | bytes 442376 | tf_op jit(solution)/shard_map/ppermute | solution.py:242
  57.2 1.6 collective-permute-start.13
  58.7 1.1 copy-done.3
  59.9 7.9 %shard_map.111 = (bf16[448,8192]{1,0:T(8,128)(2,1)}, f32[448,8192]{1,0:T(8,128)}, f32[448,8192]{1,0:T(8,128)}, f32[8,128]{1,0:T(8,128)}) custom-call(s32[1]{0:T(128)} %bitcast.42.base, bf16[448,8192]{1,0:T(8,128)(2,1)} %bitcast.80, bf16[448,8192]{1,0:T(8,128)(2,1)} %collective-permute-done.1.refs_1_, bf16[80,8192]{1,0:T(8,128)(2,1)} %copy-done.3, ...), custom_call_target="tpu_custom_call" | custom-call | flops 26214400 | bytes 17039360 | tf_op jit(solution)/shard_map/pallas_call | solution.py:163
  68.6 2.5 %copy.93.refs_5_ = bf16[8192,128]{1,0:T(8,128)(2,1)} copy(bf16[8192,128]{0,1:T(8,128)(2,1)S(1)} %bitcast.85) | data formatting | bytes 4194304 | tf_op jit(solution)/shard_map/jit(_where)/select_n | solution.py:194
  71.2 0.7 tile.9.refs_6_
  71.9 8.8 %shard_map.112 = (bf16[448,8192]{1,0:T(8,128)(2,1)}, f32[448,8192]{1,0:T(8,128)}, f32[448,8192]{1,0:T(8,128)}, f32[80,32]{1,0:T(8,128)}, f32[8,128]{1,0:T(8,128)}) custom-call(s32[1]{0:T(128)} %bitcast.30.base, bf16[80,8192]{1,0:T(8,128)(2,1)} %copy-done, ...), custom_call_target="tpu_custom_call", output_to_operand_aliasing={{0}: (8, {}), {1}: (9, {}), {2}: (10, {})} | custom-call | flops 68157440 | bytes 15728640 | tf_op jit(solution)/shard_map/pallas_call | solution.py:163
  80.8 1.6 collective-permute-start.12
  82.4 7.0 %shard_map.113 = (bf16[448,8192]{1,0:T(8,128)(2,1)}, f32[448,8192]{1,0:T(8,128)}, f32[448,8192]{1,0:T(8,128)}, f32[48,32]{1,0:T(8,128)}, f32[8,128]{1,0:T(8,128)}) custom-call(s32[1]{0:T(128)} %bitcast.43.base, bf16[48,8192]{1,0:T(8,128)(2,1)} %get-tuple-element.77.refs_0_, ...), custom_call_target="tpu_custom_call", output_to_operand_aliasing={{0}: (8, {}), {1}: (9, {}), {2}: (10, {})} | custom-call | flops 40894464 | bytes 9437184 | tf_op jit(solution)/shard_map/pallas_call | solution.py:163
  89.4 0.9 copy-done.7
  90.3 5.8 %shard_map.114 = (bf16[448,8192]{1,0:T(8,128)(2,1)}, f32[448,8192]{1,0:T(8,128)}, f32[448,8192]{1,0:T(8,128)}, f32[8,128]{1,0:T(8,128)}) custom-call(s32[1]{0:T(128)} %bitcast.29.base, bf16[448,8192]{1,0:T(8,128)(2,1)} %bitcast.81, bf16[448,8192]{1,0:T(8,128)(2,1)} %collective-permute-done.1.refs_1_, ...), custom_call_target="tpu_custom_call", output_to_operand_aliasing={{0}: (7, {}), {1}: (8, {}), {2}: (9, {})} | custom-call | flops 15728640 | bytes 10223616 | tf_op jit(solution)/shard_map/pallas_call | solution.py:163
  96.2 4.6 %collective-permute-done.12.refs_1_ = bf16[48,8192]{1,0:T(8,128)(2,1)S(1)} collective-permute-done((bf16[48,8192]{1,0:T(8,128)(2,1)S(1)}, bf16[48,8192]{1,0:T(8,128)(2,1)S(1)}, u32[]{:S(2)}, u32[]{:S(2)}) %collective-permute-start.12) | collective-permute-done | bytes 786464 | tf_op jit(solution)/shard_map/ppermute | solution.py:278
  100.8 1.6 collective-permute-start.11
  102.3 7.0 %shard_map.115 = (bf16[448,8192]{1,0:T(8,128)(2,1)}, f32[448,8192]{1,0:T(8,128)}, f32[448,8192]{1,0:T(8,128)}, f32[48,32]{1,0:T(8,128)}, f32[8,128]{1,0:T(8,128)}) custom-call(s32[1]{0:T(128)} %bitcast.44.base, bf16[48,8192]{1,0:T(8,128)(2,1)} %copy-done.1, bf16[48,8192]{1,0:T(8,128)(2,1)} %copy-done.5, ...), custom_call_target="tpu_custom_call", output_to_operand_aliasing={{0}: (8, {}), {1}: (9, {}), {2}: (10, {})} | custom-call | flops 40894464 | bytes 9437184 | tf_op jit(solution)/shard_map/pallas_call | solution.py:163
  109.4 0.9 copy-done.6
  110.3 5.9 %shard_map.116 = (bf16[448,8192]{1,0:T(8,128)(2,1)}, f32[448,8192]{1,0:T(8,128)}, f32[448,8192]{1,0:T(8,128)}, f32[8,128]{1,0:T(8,128)}) custom-call(s32[1]{0:T(128)} %bitcast.28.base, bf16[448,8192]{1,0:T(8,128)(2,1)} %bitcast.82, bf16[448,8192]{1,0:T(8,128)(2,1)} %collective-permute-done.1.refs_1_, ...), custom_call_target="tpu_custom_call", output_to_operand_aliasing={{0}: (7, {}), {1}: (8, {}), {2}: (9, {})} | custom-call | flops 15728640 | bytes 10223616 | tf_op jit(solution)/shard_map/pallas_call | solution.py:163
  116.4 0.7 collective-permute-start.10
  117.2 6.1 %shard_map.117 = (bf16[448,8192]{1,0:T(8,128)(2,1)}, f32[448,8192]{1,0:T(8,128)}, f32[448,8192]{1,0:T(8,128)}, f32[32,32]{1,0:T(8,128)}, f32[8,128]{1,0:T(8,128)}) custom-call(s32[1]{0:T(128)} %bitcast.45.base, bf16[32,8192]{1,0:T(8,128)(2,1)} %copy-done.2, bf16[32,8192]{1,0:T(8,128)(2,1)} %copy-done.8, ...), custom_call_target="tpu_custom_call", output_to_operand_aliasing={{0}: (8, {}), {1}: (9, {}), {2}: (10, {})} | custom-call | flops 27262976 | bytes 6291456 | tf_op jit(solution)/shard_map/pallas_call | solution.py:163
  123.3 0.8 copy-done.9
  124.1 5.2 %shard_map.118 = (bf16[448,8192]{1,0:T(8,128)(2,1)}, f32[448,8192]{1,0:T(8,128)}, f32[448,8192]{1,0:T(8,128)}, f32[8,128]{1,0:T(8,128)}) custom-call(s32[1]{0:T(128)} %bitcast.27.base, bf16[448,8192]{1,0:T(8,128)(2,1)} %bitcast.83, bf16[448,8192]{1,0:T(8,128)(2,1)} %collective-permute-done.1.refs_1_, ...), custom_call_target="tpu_custom_call", output_to_operand_aliasing={{0}: (7, {}), {1}: (8, {}), {2}: (9, {})} | custom-call | flops 10485760 | bytes 6815744 | tf_op jit(solution)/shard_map/pallas_call | solution.py:163
  130.0 5.2 %shard_map.119 = (bf16[448,8192]{1,0:T(8,128)(2,1)}, f32[448,8192]{1,0:T(8,128)}, f32[448,8192]{1,0:T(8,128)}, f32[16,32]{1,0:T(8,128)}, f32[8,128]{1,0:T(8,128)}) custom-call(s32[1]{0:T(128)} %bitcast.46.base, bf16[16,8192]{1,0:T(8,128)(2,1)} %bitcast_add_fusion.4.refs_0_, ...), custom_call_target="tpu_custom_call", output_to_operand_aliasing={{0}: (8, {}), {1}: (9, {}), {2}: (10, {})} | custom-call | flops 13631488 | bytes 3145728 | tf_op jit(solution)/shard_map/pallas_call | solution.py:163
  135.2 0.7 convert.22
  136.1 0.6 reshape.157
  136.7 6.5 %all-to-all-start = ((bf16[16,2,224]{2,1,0:T(2,128)(2,1)}), bf16[16,2,224]{2,1,0:T(2,128)(2,1)S(1)}, u32[]{:S(2)}, u32[]{:S(2)}) async-start(bf16[16,2,224]{2,1,0:T(2,128)(2,1)} %reshape.157), calls=%async_computation | async-start | bytes 32768 | tf_op jit(solution)/shard_map/all_to_all | solution.py:343
  143.2 6.5 %all-to-all-done = bf16[16,2,224]{2,1,0:T(2,128)(2,1)S(1)} async-done(((bf16[16,2,224]{2,1,0:T(2,128)(2,1)}), bf16[16,2,224]{2,1,0:T(2,128)(2,1)S(1)}, u32[]{:S(2)}, u32[]{:S(2)}) %all-to-all-start) | async-done | bytes 14368 | tf_op jit(solution)/shard_map/all_to_all | solution.py:343
  149.7 0.7 reshape.159
  150.4 0.7 copy-done.11
  151.1 4.4 %shard_map.120 = (bf16[448,8192]{1,0:T(8,128)(2,1)}, f32[448,8192]{1,0:T(8,128)}, f32[448,8192]{1,0:T(8,128)}, f32[8,128]{1,0:T(8,128)}) custom-call(s32[1]{0:T(128)} %bitcast.base, bf16[448,8192]{1,0:T(8,128)(2,1)} %bitcast.84, bf16[448,8192]{1,0:T(8,128)(2,1)} %collective-permute-done.1.refs_1_, ...), custom_call_target="tpu_custom_call", output_to_operand_aliasing={{0}: (7, {}), {1}: (8, {}), {2}: (9, {})} | custom-call | flops 5242880 | bytes 3407872 | tf_op jit(solution)/shard_map/pallas_call | solution.py:163
  (96 shorter events, 5.3 us)
Async XLA Ops:
  2.0 6.0 %collective-permute-start = (bf16[80,8192]{1,0:T(8,128)(2,1)S(1)}, bf16[80,8192]{1,0:T(8,128)(2,1)S(1)}, u32[]{:S(2)}, u32[]{:S(2)}) collective-permute-start(bf16[80,8192]{1,0:T(8,128)(2,1)S(1)} %dynamic-slice_bitcast_fusion), channel_id=1, source_target_pairs={{0,8},{8,0},{16,24},{24,16},{1,9},{9,1},{17,25},{25,17},{2,10},{10... | collective-permute-start | bytes 3932168 | tf_op jit(solution)/shard_map/ppermute | solution.py:277
  2.6 7.1 %collective-permute-start.2 = (bf16[2,3584]{1,0:T(2,128)(2,1)}, bf16[2,3584]{1,0:T(2,128)(2,1)S(1)}, u32[]{:S(2)}, u32[]{:S(2)}) collective-permute-start(bf16[2,3584]{1,0:T(2,128)(2,1)} %param.13), channel_id=1, source_target_pairs={{0,1},{1,0},{2,3},{3,2},{4,5},{5,4},{6,7},{7,6},{8,9},{9,8},{10,11... | collective-permute-start | bytes 43016 | tf_op jit(solution)/shard_map/ppermute | solution.py:242
  5.2 4.5 %collective-permute-start.3 = (bf16[2,3584]{1,0:T(2,128)(2,1)}, bf16[2,3584]{1,0:T(2,128)(2,1)S(1)}, u32[]{:S(2)}, u32[]{:S(2)}) collective-permute-start(bf16[2,3584]{1,0:T(2,128)(2,1)} %param.13), channel_id=1, source_target_pairs={{0,8},{1,9},{2,10},{3,11},{4,12},{5,13},{6,14},{7,15},{8,0},{9,1},... | collective-permute-start | bytes 43016 | tf_op jit(solution)/shard_map/ppermute | solution.py:242
  5.3 4.4 %collective-permute-start.4 = (bf16[2,3584]{1,0:T(2,128)(2,1)}, bf16[2,3584]{1,0:T(2,128)(2,1)S(1)}, u32[]{:S(2)}, u32[]{:S(2)}) collective-permute-start(bf16[2,3584]{1,0:T(2,128)(2,1)} %param.13), channel_id=1, source_target_pairs={{0,9},{1,8},{2,11},{3,10},{4,13},{5,12},{6,15},{7,14},{8,1},{9,0},... | collective-permute-start | bytes 43016 | tf_op jit(solution)/shard_map/ppermute | solution.py:242
  6.8 1.2 collective-permute-start.8
  9.7 22.4 %copy-start = (bf16[80,8192]{1,0:T(8,128)(2,1)}, bf16[80,8192]{1,0:T(8,128)(2,1)S(1)}, u32[]{:S(2)}) copy-start(bf16[80,8192]{1,0:T(8,128)(2,1)S(1)} %bitcast_add_fusion.refs_0_) | copy-start | bytes 3932164
  9.8 36.5 %collective-permute-start.1 = (bf16[448,8192]{1,0:T(8,128)(2,1)}, bf16[448,8192]{1,0:T(8,128)(2,1)}, u32[]{:S(2)}, u32[]{:S(2)}) collective-permute-start(bf16[448,8192]{1,0:T(8,128)(2,1)} %bitcast.79), channel_id=1, source_target_pairs={{0,8},{8,0},{16,24},{24,16},{1,9},{9,1},{17,25},{25,17},{2,10},{10... | collective-permute-start | bytes 22020104 | tf_op jit(solution)/shard_map/ppermute | solution.py:277
  11.1 6.3 %collective-permute-start.5 = (bf16[2,2,2,3584]{3,2,1,0:T(2,128)(2,1)S(1)}, bf16[2,2,2,3584]{3,2,1,0:T(2,128)(2,1)S(1)}, u32[]{:S(2)}, u32[]{:S(2)}) collective-permute-start(bf16[2,2,2,3584]{3,2,1,0:T(2,128)(2,1)S(1)} %broadcast_select_fusion.4), channel_id=1, source_target_pairs={{0,2},{1,3},{2,0},{3,1},{4,6},{5,7},{6,4},{7,5},{8,10},{9,11},{10,... | collective-permute-start | bytes 172040 | tf_op jit(solution)/shard_map/ppermute | solution.py:242
  13.0 6.5 %collective-permute-start.6 = (bf16[2,2,2,3584]{3,2,1,0:T(2,128)(2,1)S(1)}, bf16[2,2,2,3584]{3,2,1,0:T(2,128)(2,1)S(1)}, u32[]{:S(2)}, u32[]{:S(2)}) collective-permute-start(bf16[2,2,2,3584]{3,2,1,0:T(2,128)(2,1)S(1)} %broadcast_select_fusion.4), channel_id=1, source_target_pairs={{0,4},{1,5},{2,6},{3,7},{4,0},{5,1},{6,2},{7,3},{8,12},{9,13},{10,... | collective-permute-start | bytes 172040 | tf_op jit(solution)/shard_map/ppermute | solution.py:242
  15.6 6.0 %collective-permute-start.7 = (bf16[2,2,2,3584]{3,2,1,0:T(2,128)(2,1)S(1)}, bf16[2,2,2,3584]{3,2,1,0:T(2,128)(2,1)S(1)}, u32[]{:S(2)}, u32[]{:S(2)}) collective-permute-start(bf16[2,2,2,3584]{3,2,1,0:T(2,128)(2,1)S(1)} %broadcast_select_fusion.4), channel_id=1, source_target_pairs={{0,6},{1,7},{2,4},{3,5},{4,2},{5,3},{6,0},{7,1},{8,14},{9,15},{10,... | collective-permute-start | bytes 172040 | tf_op jit(solution)/shard_map/ppermute | solution.py:242
  15.7 30.6 %collective-permute-start.14 = (bf16[80,8192]{1,0:T(8,128)(2,1)S(1)}, bf16[80,8192]{1,0:T(8,128)(2,1)}, u32[]{:S(2)}, u32[]{:S(2)}) collective-permute-start(bf16[80,8192]{1,0:T(8,128)(2,1)S(1)} %bitcast_add_fusion.refs_0_), channel_id=1, source_target_pairs={{0,16},{8,24},{16,0},{24,8},{1,17},{9,25},{17,1},{25,9},{2,18},{10... | collective-permute-start | bytes 3932168 | tf_op jit(solution)/shard_map/ppermute | solution.py:278
  32.2 4.4 %collective-permute-start.9 = (bf16[32,1152]{1,0:T(8,128)(2,1)S(1)}, bf16[32,1152]{1,0:T(8,128)(2,1)S(1)}, u32[]{:S(2)}, u32[]{:S(2)}) collective-permute-start(bf16[32,1152]{1,0:T(8,128)(2,1)S(1)} %get-tuple-element.135), channel_id=1, source_target_pairs={{0,1},{1,0},{2,3},{3,2},{4,5},{5,4},{6,7},{7,6},{8,9},{9,8},{10,11... | collective-permute-start | bytes 221192 | tf_op jit(solution)/shard_map/ppermute | solution.py:242
  46.3 12.5 %collective-permute-start.18 = (bf16[80,8192]{1,0:T(8,128)(2,1)}, bf16[80,8192]{1,0:T(8,128)(2,1)S(1)}, u32[]{:S(2)}, u32[]{:S(2)}) collective-permute-start(bf16[80,8192]{1,0:T(8,128)(2,1)} %collective-permute-done.14.refs_1_), channel_id=1, source_target_pairs={{0,8},{8,0},{16,24},{24,16},{1,9},{9,1},{17,25},{25,17},{2,10},{10... | collective-permute-start | bytes 3932168 | tf_op jit(solution)/shard_map/ppermute | solution.py:277
  47.6 53.2 %copy-start.2 = (bf16[32,8192]{1,0:T(8,128)(2,1)}, bf16[32,8192]{1,0:T(8,128)(2,1)S(1)}, u32[]{:S(2)}) copy-start(bf16[32,8192]{1,0:T(8,128)(2,1)S(1)} %bitcast_add_fusion.3.refs_0_) | copy-start | bytes 1572868
  52.7 28.1 %copy-start.1 = (bf16[48,8192]{1,0:T(8,128)(2,1)}, bf16[48,8192]{1,0:T(8,128)(2,1)S(1)}, u32[]{:S(2)}) copy-start(bf16[48,8192]{1,0:T(8,128)(2,1)S(1)} %get-tuple-element.76.refs_0_) | copy-start | bytes 2359300
  52.7 15.1 %collective-permute-start.15 = (bf16[2,32,1152]{2,1,0:T(8,128)(2,1)S(1)}, bf16[2,32,1152]{2,1,0:T(8,128)(2,1)S(1)}, u32[]{:S(2)}, u32[]{:S(2)}) collective-permute-start(bf16[2,32,1152]{2,1,0:T(8,128)(2,1)S(1)} %reverse_select_fusion.2), channel_id=1, source_target_pairs={{0,2},{1,3},{2,0},{3,1},{4,6},{5,7},{6,4},{7,5},{8,10},{9,11},{10,... | collective-permute-start | bytes 442376 | tf_op jit(solution)/shard_map/ppermute | solution.py:242
  53.3 14.6 %collective-permute-start.16 = (bf16[2,32,1152]{2,1,0:T(8,128)(2,1)S(1)}, bf16[2,32,1152]{2,1,0:T(8,128)(2,1)S(1)}, u32[]{:S(2)}, u32[]{:S(2)}) collective-permute-start(bf16[2,32,1152]{2,1,0:T(8,128)(2,1)S(1)} %reverse_select_fusion.2), channel_id=1, source_target_pairs={{0,4},{1,5},{2,6},{3,7},{4,0},{5,1},{6,2},{7,3},{8,12},{9,13},{10,... | collective-permute-start | bytes 442376 | tf_op jit(solution)/shard_map/ppermute | solution.py:242
  56.8 11.1 %collective-permute-start.17 = (bf16[2,32,1152]{2,1,0:T(8,128)(2,1)S(1)}, bf16[2,32,1152]{2,1,0:T(8,128)(2,1)S(1)}, u32[]{:S(2)}, u32[]{:S(2)}) collective-permute-start(bf16[2,32,1152]{2,1,0:T(8,128)(2,1)S(1)} %reverse_select_fusion.2), channel_id=1, source_target_pairs={{0,6},{1,7},{2,4},{3,5},{4,2},{5,3},{6,0},{7,1},{8,14},{9,15},{10,... | collective-permute-start | bytes 442376 | tf_op jit(solution)/shard_map/ppermute | solution.py:242
  57.2 23.6 %collective-permute-start.13 = (bf16[48,8192]{1,0:T(8,128)(2,1)}, bf16[48,8192]{1,0:T(8,128)(2,1)}, u32[]{:S(2)}, u32[]{:S(2)}) collective-permute-start(bf16[48,8192]{1,0:T(8,128)(2,1)} %get-tuple-element.77.refs_0_), channel_id=1, source_target_pairs={{0,16},{8,24},{16,0},{24,8},{1,17},{9,25},{17,1},{25,9},{2,18},{10... | collective-permute-start | bytes 2359304 | tf_op jit(solution)/shard_map/ppermute | solution.py:278
  58.7 1.2 copy-start.3
  80.8 8.7 %collective-permute-start.19 = (bf16[48,8192]{1,0:T(8,128)(2,1)}, bf16[48,8192]{1,0:T(8,128)(2,1)S(1)}, u32[]{:S(2)}, u32[]{:S(2)}) collective-permute-start(bf16[48,8192]{1,0:T(8,128)(2,1)} %collective-permute-done.13.refs_1_), channel_id=1, source_target_pairs={{0,8},{8,0},{16,24},{24,16},{1,9},{9,1},{17,25},{25,17},{2,10},{10... | collective-permute-start | bytes 2359304 | tf_op jit(solution)/shard_map/ppermute | solution.py:277
  80.8 19.9 %collective-permute-start.12 = (bf16[48,8192]{1,0:T(8,128)(2,1)S(1)}, bf16[48,8192]{1,0:T(8,128)(2,1)S(1)}, u32[]{:S(2)}, u32[]{:S(2)}) collective-permute-start(bf16[48,8192]{1,0:T(8,128)(2,1)S(1)} %get-tuple-element.76.refs_0_), channel_id=1, source_target_pairs={{0,16},{8,24},{16,0},{24,8},{1,17},{9,25},{17,1},{25,9},{2,18},{10... | collective-permute-start | bytes 2359304 | tf_op jit(solution)/shard_map/ppermute | solution.py:278
  89.4 0.9 copy-start.7
  100.8 1.6 %copy-start.5 = (bf16[48,8192]{1,0:T(8,128)(2,1)}, bf16[48,8192]{1,0:T(8,128)(2,1)S(1)}, u32[]{:S(2)}) copy-start(bf16[48,8192]{1,0:T(8,128)(2,1)S(1)} %collective-permute-done.12.refs_1_) | copy-start | bytes 2359300
  100.8 8.6 %collective-permute-start.20 = (bf16[48,8192]{1,0:T(8,128)(2,1)S(1)}, bf16[48,8192]{1,0:T(8,128)(2,1)S(1)}, u32[]{:S(2)}, u32[]{:S(2)}) collective-permute-start(bf16[48,8192]{1,0:T(8,128)(2,1)S(1)} %collective-permute-done.12.refs_1_), channel_id=1, source_target_pairs={{0,8},{8,0},{16,24},{24,16},{1,9},{9,1},{17,25},{25,17},{2,10},{10... | collective-permute-start | bytes 2359304 | tf_op jit(solution)/shard_map/ppermute | solution.py:277
  100.8 15.4 %collective-permute-start.11 = (bf16[32,8192]{1,0:T(8,128)(2,1)S(1)}, bf16[32,8192]{1,0:T(8,128)(2,1)S(1)}, u32[]{:S(2)}, u32[]{:S(2)}) collective-permute-start(bf16[32,8192]{1,0:T(8,128)(2,1)S(1)} %bitcast_add_fusion.3.refs_0_), channel_id=1, source_target_pairs={{0,16},{8,24},{16,0},{24,8},{1,17},{9,25},{17,1},{25,9},{2,18},{10... | collective-permute-start | bytes 1572872 | tf_op jit(solution)/shard_map/ppermute | solution.py:278
  109.4 0.9 copy-start.6
  110.3 6.1 %copy-start.4 = (bf16[16,8192]{1,0:T(8,128)(2,1)S(1)}, bf16[16,8192]{1,0:T(8,128)(2,1)}, u32[]{:S(2)}) copy-start(bf16[16,8192]{1,0:T(8,128)(2,1)} %bitcast_add_fusion.4.refs_0_) | copy-start | bytes 786436
  116.2 1.0 copy-start.8
  116.2 7.1 %collective-permute-start.21 = (bf16[32,8192]{1,0:T(8,128)(2,1)S(1)}, bf16[32,8192]{1,0:T(8,128)(2,1)S(1)}, u32[]{:S(2)}, u32[]{:S(2)}) collective-permute-start(bf16[32,8192]{1,0:T(8,128)(2,1)S(1)} %collective-permute-done.11.refs_1_), channel_id=1, source_target_pairs={{0,8},{8,0},{16,24},{24,16},{1,9},{9,1},{17,25},{25,17},{2,10},{10... | collective-permute-start | bytes 1572872 | tf_op jit(solution)/shard_map/ppermute | solution.py:277
  116.4 12.9 %collective-permute-start.10 = (bf16[16,8192]{1,0:T(8,128)(2,1)S(1)}, bf16[16,8192]{1,0:T(8,128)(2,1)S(1)}, u32[]{:S(2)}, u32[]{:S(2)}) collective-permute-start(bf16[16,8192]{1,0:T(8,128)(2,1)S(1)} %copy-done.4), channel_id=1, source_target_pairs={{0,16},{8,24},{16,0},{24,8},{1,17},{9,25},{17,1},{25,9},{2,18},{10... | collective-permute-start | bytes 786440 | tf_op jit(solution)/shard_map/ppermute | solution.py:278
  123.3 0.8 copy-start.9
  124.1 5.4 %copy-start.12 = (f32[80,32]{1,0:T(8,128)S(1)}, f32[80,32]{1,0:T(8,128)}, u32[]{:S(2)}) copy-start(f32[80,32]{1,0:T(8,128)} %get-tuple-element.127) | copy-start | bytes 30724
  124.1 5.5 %copy-start.13 = (f32[48,32]{1,0:T(8,128)S(1)}, f32[48,32]{1,0:T(8,128)}, u32[]{:S(2)}) copy-start(f32[48,32]{1,0:T(8,128)} %get-tuple-element.128) | copy-start | bytes 18436
  124.1 5.6 %copy-start.14 = (f32[48,32]{1,0:T(8,128)S(1)}, f32[48,32]{1,0:T(8,128)}, u32[]{:S(2)}) copy-start(f32[48,32]{1,0:T(8,128)} %get-tuple-element.129) | copy-start | bytes 18436
  124.1 5.7 %copy-start.15 = (f32[32,32]{1,0:T(8,128)S(1)}, f32[32,32]{1,0:T(8,128)}, u32[]{:S(2)}) copy-start(f32[32,32]{1,0:T(8,128)} %get-tuple-element.130) | copy-start | bytes 12292
  129.3 0.7 copy-start.10
  129.3 21.1 %collective-permute-start.22 = (bf16[16,8192]{1,0:T(8,128)(2,1)S(1)}, bf16[16,8192]{1,0:T(8,128)(2,1)S(1)}, u32[]{:S(2)}, u32[]{:S(2)}) collective-permute-start(bf16[16,8192]{1,0:T(8,128)(2,1)S(1)} %collective-permute-done.10.refs_1_), channel_id=1, source_target_pairs={{0,8},{8,0},{16,24},{24,16},{1,9},{9,1},{17,25},{25,17},{2,10},{10... | collective-permute-start | bytes 786440 | tf_op jit(solution)/shard_map/ppermute | solution.py:277
  136.7 13.0 %all-to-all-start = ((bf16[16,2,224]{2,1,0:T(2,128)(2,1)}), bf16[16,2,224]{2,1,0:T(2,128)(2,1)S(1)}, u32[]{:S(2)}, u32[]{:S(2)}) async-start(bf16[16,2,224]{2,1,0:T(2,128)(2,1)} %reshape.157), calls=%async_computation | async-start | bytes 32768 | tf_op jit(solution)/shard_map/all_to_all | solution.py:343
  150.4 0.7 copy-start.11
where the time goes:
time: 156 us
  Pallas kernels  63.3 us (41%)
  starting transfers between devices  28.8 us (18%)
  waiting for transfers between devices  28.6 us (18%)
  other arithmetic  12.7 us (8%)
  local copies, waits for them, and re-layouts  11.5 us (7%)
  matrix products  9.48 us (6%)
    pallas_call x10, Pallas kernels, adam_rows(): pl.pallas_call(functools.partial(adam_kernel, (len(whole), len(local)), b...  63.3 us
    ppermute x5, waiting for transfers between devices, body(): lax.ppermute(a, 'wide', [(i, i ^ 2) for i in range(wide)])  14.2 us
    ppermute x11, starting transfers between devices, xor_gather(): lax.ppermute(x, axes, [(i, i ^ m) for i in range(size)])  13.7 us
    dot_general x1, matrix products, up_project(): jnp.einsum('td,dgu->gtu', rows, gate_up, preferred_element_type=jnp.float32)  9.48 us
    ppermute x11, waiting for transfers between devices, xor_gather(): lax.ppermute(x, axes, [(i, i ^ m) for i in range(size)])  7.89 us
    ppermute x5, starting transfers between devices, body(): lax.ppermute(a, 'wide', [(i, i ^ 2) for i in range(wide)])  7.19 us
    all_to_all x1, starting transfers between devices, body(): out = lax.all_to_all(out, both, 0, 0, axis_index_groups=groups, tiled=True)  6.49 us
    all_to_all x1, waiting for transfers between devices, body(): out = lax.all_to_all(out, both, 0, 0, axis_index_groups=groups, tiled=True)  6.46 us
  transfers between devices with their start and end apart: 24, of which 8 were waited for; matrix products, arithmetic and copies ran while one was open for 18% of the time, Pallas kernels for 38%

commit v1 on v0

v1 whole, which is shorter than its diff:
```python
import functools

import jax
import jax.numpy as jnp
from jax import lax
from jax.experimental import pallas as pl
from jax.experimental.pallas import tpu as pltpu
from jax.sharding import PartitionSpec as P


EXPERTS = 8
QBLOCK = 128
LANES = 128
VMEM_GRANT = 40 << 20

beta_first = 0.9
beta_second = 0.95
learn_rate = 0.003
adam_eps = 1e-08
quant_limit = 448.0
amax_eps = 1e-06
bias_first = 1.0 - 0.9**10
bias_second = 1.0 - 0.95**10


def adam_kernel(shared, runs, block, down, aliased, base, *refs):
    refs = list(refs)
    whole = [refs.pop(0) for _ in range(shared)]
    local = [[refs.pop(0) for _ in range(own)] for _, own, _ in runs]
    state = [refs.pop(0) for _ in range(3)]
    counts = [rows for rows, _, _ in runs]
    if down:
        hidden, weight = [refs.pop(0) for _ in range(down)], refs.pop(0)
    refs = refs[4 if aliased else 0 :]
    fresh = [refs.pop(0) for _ in range(3)]
    comb = refs.pop(0) if down else None
    token = refs.pop(0)
    term_v = [refs.pop(0) for _ in range(3)]
    state_v = [refs.pop(0) for _ in range(3)]
    acc = refs.pop(0) if down else None
    in_sem, out_sem = refs
    cols = state_v[0].shape[1]
    toks = comb.shape[0] if down else 0

    def copies(run, j):
        slot = sum(counts[:run]) // block + j
        there = pl.ds(pl.multiple_of(base[run] + j * block, 8), block)
        here = pl.ds(pl.multiple_of(slot * block, 8), block)
        near = pl.ds(pl.multiple_of(j * block, 8), block)
        far = () if runs[run][2] and local[run] else whole
        pairs = [(a.at[there], v) for a, v in zip(far, term_v)]
        pairs += [(a.at[near], v) for a, v in zip(local[run], term_v[len(far) :])]
        pairs += [(a.at[there], v) for a, v in zip(state, state_v)]
        ins = [
            pltpu.make_async_copy(a, v.at[here], in_sem.at[q, slot]) for q, (a, v) in enumerate(pairs)
        ]
        outs = [
            pltpu.make_async_copy(v.at[here], f.at[there], out_sem.at[q, slot])
            for q, (v, f) in enumerate(zip(state_v, fresh))
        ]
        return ins, outs, here

    def begin(run, j, carry):
        for copy in copies(run, j)[0]:
            copy.start()
        return carry

    def adam(terms, here, at):
        read = lambda ref: ref[here, at].astype(jnp.float32)
        grad = read(term_v[0])
        if terms == 3:
            grad = (grad + read(term_v[1])).astype(jnp.bfloat16).astype(jnp.float32)
        if terms > 1:
            grad = grad + read(term_v[terms - 1])
        first = beta_first * read(state_v[1]) + (1.0 - beta_first) * grad
        second = beta_second * read(state_v[2]) + (1.0 - beta_second) * grad * grad
        state_v[1][here, at] = first
        state_v[2][here, at] = second
        spread = second * (1.0 / bias_second)
        step = first * (learn_rate / bias_first) / (spread * lax.rsqrt(spread) + adam_eps)
        updated = read(state_v[0]) - step
        state_v[0][here, at] = updated.astype(jnp.bfloat16)
        return updated

    def step_down(terms, here):
        slices = weight.shape[0]
        unit = cols // slices
        total = jnp.zeros((block, toks), jnp.float32)
        for s in range(slices):
            updated = adam(terms, here, slice(s * unit, (s + 1) * unit))
            partial = jnp.zeros((block, toks), jnp.float32)
            for b in range(unit // QBLOCK):
                cut = slice(b * QBLOCK, (b + 1) * QBLOCK)
                cells = updated[:, cut]
                amax = jnp.max(jnp.abs(cells), axis=1, keepdims=True)
                scale = (amax + amax_eps) * (1.0 / quant_limit)
                scale = scale.astype(jnp.bfloat16).astype(jnp.float32)
                quanta = (cells * (1.0 / scale)).astype(jnp.bfloat16)
                dots = lax.dot_general(
                    quanta,
                    jnp.concatenate([h[s, :, cut] for h in hidden], axis=0),
                    (((1,), (1,)), ((), ())),
                    preferred_element_type=jnp.float32,
                )
                partial = partial + scale * dots
            total = total + partial.astype(jnp.bfloat16).astype(jnp.float32) * weight[s : s + 1, :]
        acc[here, :] = total

    def step_plain(terms, here):
        width = 1024 if cols % 1024 == 0 else LANES

        def part(c, carry):
            adam(terms, here, pl.ds(pl.multiple_of(c * width, LANES), width))
            return carry

        lax.fori_loop(0, cols // width, part, 0)

    def step(run, j, carry):
        ins, outs, here = copies(run, j)
        for copy in ins:
            copy.wait()
        _, own, products = runs[run]
        terms = own + (0 if products and own else shared)
        (step_down if products else step_plain)(terms, here)
        for copy in outs:
            copy.start()
        return carry

    def finish(run, j, carry):
        for copy in copies(run, j)[1]:
            copy.wait()
        return carry

    token[...] = jnp.zeros_like(token)
    for phase in (begin, step, finish):
        for run, rows in enumerate(counts):
            lax.fori_loop(0, rows // block, functools.partial(phase, run), 0)
        if phase is step and down:
            ones = (
                lax.broadcasted_iota(jnp.int32, (toks, toks), 0)
                == lax.broadcasted_iota(jnp.int32, (toks, toks), 1)
            ).astype(jnp.bfloat16)
            comb[...] = lax.dot_general(
                ones,
                acc[: comb.shape[1], :].astype(jnp.bfloat16),
                (((1,), (1,)), ((), ())),
                preferred_element_type=jnp.float32,
            ).astype(jnp.bfloat16)


def adam_rows(runs, whole, state, outs, token, block, hidden=(), weight=None):
    full, cols = state[0].shape
    counts = [count for _, count, _, _ in runs]
    rows = sum(counts)
    made = sum(count for _, count, _, products in runs if products)
    down = len(hidden)
    toks = sum(h.shape[1] for h in hidden)
    hbm, vmem = pl.BlockSpec(memory_space=pltpu.HBM), pl.BlockSpec(memory_space=pltpu.VMEM)
    parts = [a for _, _, own, _ in runs for a in own]
    far = lambda a: pltpu.with_memory_space_constraint(a, pltpu.HBM)
    args = [*map(far, whole), *parts, *map(far, state)]
    in_specs = [hbm] * len(whole) + [pl.BlockSpec(memory_space=pl.ANY)] * len(parts)
    in_specs += [hbm] * len(state)
    if down:
        args += [*hidden, weight]
        in_specs += [vmem] * (down + 1)
    aliases = {}
    if outs is not None:
        aliases = {1 + len(args) + i: i for i in range(3)}
        in_specs += [hbm] * 3 + [vmem]
        args += [*outs, token]
    cells = rows * cols
    scratch = [pltpu.VMEM((rows, cols), jnp.bfloat16)] * 4
    scratch += [pltpu.VMEM((rows, cols), jnp.float32)] * 2
    if down:
        scratch.append(pltpu.VMEM((rows, toks), jnp.float32))
    scratch += [
        pltpu.SemaphoreType.DMA((6, rows // block)),
        pltpu.SemaphoreType.DMA((3, rows // block)),
    ]
    result = pl.pallas_call(
        functools.partial(
            adam_kernel,
            len(whole),
            tuple((count, len(own), products) for _, count, own, products in runs),
            block,
            down,
            outs is not None,
        ),
        grid_spec=pltpu.PrefetchScalarGridSpec(
            num_scalar_prefetch=1,
            grid=(),
            in_specs=in_specs,
            out_specs=[hbm] * 3 + [vmem] * (1 + bool(down)),
            scratch_shapes=scratch,
        ),
        out_shape=[
            jax.ShapeDtypeStruct((full, cols), jnp.bfloat16),
            jax.ShapeDtypeStruct((full, cols), jnp.float32),
            jax.ShapeDtypeStruct((full, cols), jnp.float32),
        ]
        + [jax.ShapeDtypeStruct((toks, made), jnp.bfloat16)] * bool(down)
        + [jax.ShapeDtypeStruct((8, LANES), jnp.float32)],
        input_output_aliases=aliases,
        compiler_params=pltpu.CompilerParams(vmem_limit_bytes=VMEM_GRANT),
        cost_estimate=pl.CostEstimate(
            flops=cells * (40 + 2 * toks),
            bytes_accessed=cells * 26,
            transcendentals=cells * 3,
        ),
    )(jnp.stack([run[0] for run in runs]).astype(jnp.int32), *args)
    return result[:3], result[-1], result[3]


def token_weights(expert_ids, gate_vals):
    onehot = (expert_ids[:, :, None] == jnp.arange(EXPERTS, dtype=jnp.int32)).astype(jnp.float32)
    return jnp.sum(onehot * gate_vals.astype(jnp.float32)[:, :, None], axis=1).astype(jnp.bfloat16)


def up_project(rows, gate_up):
    proj = jnp.einsum("td,dgu->gtu", rows, gate_up, preferred_element_type=jnp.float32)
    return (jax.nn.silu(proj[0]) * proj[1]).astype(jnp.bfloat16)


def plain_body(grads, state, gate_up, tokens, expert_ids, gate_vals):
    narrow = lax.axis_size("narrow")
    tok_count, width = tokens.shape
    full = grads.shape[0]
    spread = lambda x: lax.all_to_all(
        jnp.broadcast_to(x[None], (narrow,) + x.shape), "narrow", 0, 0, tiled=True
    )
    total = lax.psum(grads, "wide")
    local = jnp.pad(token_weights(expert_ids, gate_vals), ((0, 0), (0, LANES - EXPERTS)))
    toks = narrow * tok_count
    every = spread(jnp.concatenate([tokens, local], axis=1)).reshape(toks, -1)
    hidden = spread(up_project(every[:, :width], gate_up))
    weight = jnp.repeat(every[:, width : width + EXPERTS].T, narrow // EXPERTS, axis=0)
    weight = weight.astype(jnp.float32)
    zero = jnp.zeros((), jnp.int32)
    runs = [(zero, full, (), True)]
    outs, _, comb = adam_rows(runs, (total,), state, None, None, 8, (hidden,), weight)
    out = comb.reshape(narrow, tok_count, full)
    out = lax.all_to_all(out, "narrow", 0, 0, tiled=True)
    return (*outs, out.transpose(1, 0, 2).reshape(tok_count, narrow * full))


together = lax.optimization_barrier


def row_chunks(half):
    sizes, left = [], half
    for share in CHUNKS:
        take = min(left, max(8, half * share // sum(CHUNKS) // 16 * 16))
        sizes.append(take)
        left -= take
    sizes[0] += left
    return [n for n in sizes if n]


CHUNKS = (48, 64, 48, 32, 32)


def body(grad_parts, master, moment_one, moment_two, gate_up, tokens, expert_ids, gate_vals):
    grads = grad_parts[0]
    full, cols = grads.shape
    wide, narrow = lax.axis_size("wide"), lax.axis_size("narrow")
    state = (master, moment_one, moment_two)
    tok_count, width = tokens.shape
    if wide != 4 or narrow != 8 or full % 32:
        return plain_body(grads, state, gate_up, tokens, expert_ids, gate_vals)

    both = ("wide", "narrow")
    core = lax.axis_index("wide") & 1
    swap_core = lambda a: lax.ppermute(a, "wide", [(i, i ^ 1) for i in range(wide)])
    swap_chip = lambda a: lax.ppermute(a, "wide", [(i, i ^ 2) for i in range(wide)])
    half = full // 2
    sizes = row_chunks(half)
    starts = [sum(sizes[:k]) for k in range(len(sizes))]
    mine, theirs = core * half, (1 - core) * half

    def rows_of(a, at, n):
        tiles = lax.dynamic_slice_in_dim(a.reshape(full // 16, 16, cols), at // 16, n // 16, 0)
        return tiles.reshape(n, cols)

    lead = swap_core(rows_of(grads, theirs, sizes[0]))
    held, lead = together((grads, lead))
    other = swap_core(held)
    sums = [rows_of(grads, mine, sizes[0]) + lead]

    def send(k):
        return swap_chip(sums[k])

    got = [send(0)]
    other, sums[0] = together((other, sums[0]))
    sum_of = lambda k: rows_of(grads, mine + starts[k], sizes[k]) + rows_of(other, mine + starts[k], sizes[k])
    sums.append(sum_of(1))

    def spread(x):
        x = jnp.broadcast_to(x[None], (narrow, *x.shape))
        return lax.all_to_all(x, "narrow", 0, 0, tiled=True)

    toks = narrow * tok_count
    local = jnp.pad(token_weights(expert_ids, gate_vals), ((0, 0), (0, LANES - EXPERTS)))
    packed = jnp.concatenate([tokens, local], axis=1)
    every = spread(packed)
    every, sums[1] = together((every, sums[1]))
    got.append(send(1))
    every = every.reshape(toks, -1)
    chosen = every[:, width : width + EXPERTS]
    theirs_chosen = swap_core(chosen)
    weight = jnp.concatenate([chosen, theirs_chosen]).T.astype(jnp.float32)
    weight = jnp.repeat(weight, narrow // EXPERTS, axis=0)
    piece = up_project(every[:, :width], gate_up)
    piece, other = together((piece, other))
    hidden = spread(piece)
    for k in range(2, len(sizes)):
        sums.append(sum_of(k))
        got.append(send(k))
    hidden = (hidden, swap_core(hidden))

    outs, combs, token, relays = None, [], None, []

    def relay(k):
        nonlocal token
        if token is not None:
            got[k], token = together((got[k], token))
        relays.append(swap_core(got[k]))

    def update(own=(), rest=()):
        nonlocal outs, token
        runs = [(mine + starts[k], sizes[k], (sums[k], got[k]), True) for k in own]
        runs += [(theirs + starts[k], sizes[k], (relays[k],), False) for k in rest]
        whole = (grads, other) if rest else ()
        extra = (hidden, weight) if own else ()
        outs, token, comb = adam_rows(runs, whole, state, outs, token, 16, *extra)
        if own:
            combs.append(comb)

    relay(0)
    relays[0], weight = together((relays[0], weight))
    update(rest=(0,))
    relay(1)
    update(own=(0, 1), rest=(1,))
    relay(2)
    update(own=(2,), rest=(2,))
    for k in range(3, len(sizes)):
        relay(k)
        update(own=(k,))
        update(rest=(k,))
    out = jnp.concatenate(combs, axis=1).reshape(2, narrow, tok_count, half)
    out = jnp.where(core == 0, out, out[::-1]).reshape(2 * narrow, tok_count, half)
    groups = [[(2 * x + c) * narrow + n for c in range(2) for n in range(narrow)] for x in range(wide // 2)]
    out = lax.all_to_all(out, both, 0, 0, axis_index_groups=groups, tiled=True)
    out = out.reshape(2, narrow, tok_count, half).transpose(2, 1, 0, 3).reshape(tok_count, narrow * full)
    return (*outs, out)


def solution(mesh):
    in_specs = (
        P("wide", "narrow", None),
        P("narrow", None),
        P("narrow", None),
        P("narrow", None),
        P(None, None, "narrow"),
        P(("wide", "narrow"), None),
        P(("wide", "narrow"), None),
        P(("wide", "narrow"), None),
    )
    out_specs = (
        P("narrow", None),
        P("narrow", None),
        P("narrow", None),
        P(("wide", "narrow"), None),
    )
    return jax.shard_map(body, mesh=mesh, in_specs=in_specs, out_specs=out_specs, check_vma=False)
```

time: 156 us -> 139 us (0.89)
  Pallas kernels: 63.3 us -> 41.9 us
  blocking collectives: 0 us -> 14.9 us
  waiting for transfers between devices: 28.6 us -> 40.9 us
  starting transfers between devices: 28.8 us -> 18.4 us
  local copies, waits for them, and re-layouts: 11.5 us -> 4.21 us
  other arithmetic: 12.7 us -> 8.25 us
    pallas_call x10 -> x7, Pallas kernels: 63.3 us -> 41.9 us  [adam_rows(): pl.pallas_call(functools.partial(adam_kernel, len(whole), tuple(((count,...]
    ppermute x5, waiting for transfers between devices: 14.2 us -> 31 us  [body(): lax.ppermute(a, 'wide', [(i, i ^ 2) for i in range(wide)])]
    all_to_all x0 -> x1, blocking collectives: none -> 14.9 us  [spread(): return lax.all_to_all(x, 'narrow', 0, 0, tiled=True)]
    ppermute x11 -> x0, starting transfers between devices: 13.7 us -> none  [xor_gather(): lax.ppermute(x, axes, [(i, i ^ m) for i in range(size)])]
    ppermute x11 -> x0, waiting for transfers between devices: 7.89 us -> none  [xor_gather(): lax.ppermute(x, axes, [(i, i ^ m) for i in range(size)])]
    all_to_all x0 -> x1, starting transfers between devices: none -> 5.83 us  [spread(): return lax.all_to_all(x, 'narrow', 0, 0, tiled=True)]
    unnamed x35 -> x5, local copies, waits for them, and re-layouts: 4.72 us -> 1.22 us
    ppermute x7 -> x9, waiting for transfers between devices: 0.02 us -> 3.44 us  [body(): lax.ppermute(a, 'wide', [(i, i ^ 1) for i in range(wide)])]
  transfers between devices with their start and end apart: 24 -> 16, of which waited for: 8 -> 8; matrix products, arithmetic and copies ran while one was open for 18% -> 14% of each run, Pallas kernels for 38% -> 27%
where the time goes in v1:
time: 139 us; the launch traced here: 138 us
  Pallas kernels  41.9 us (30%)
  waiting for transfers between devices  40.9 us (29%)
  starting transfers between devices  18.4 us (13%)
  blocking collectives  14.9 us (11%)
  matrix products  8.99 us (6%)
  other arithmetic  8.25 us (6%)
  local copies, waits for them, and re-layouts  4.21 us (3%)
    pallas_call x7, Pallas kernels, adam_rows(): pl.pallas_call(functools.partial(adam_kernel, len(whole), tuple(((count,...  41.9 us
    ppermute x5, waiting for transfers between devices, body(): lax.ppermute(a, 'wide', [(i, i ^ 2) for i in range(wide)])  31 us
    all_to_all x1, blocking collectives, spread(): return lax.all_to_all(x, 'narrow', 0, 0, tiled=True)  14.9 us
    dot_general x1, matrix products, up_project(): jnp.einsum('td,dgu->gtu', rows, gate_up, preferred_element_type=jnp.float32)  8.99 us
    ppermute x5, starting transfers between devices, body(): lax.ppermute(a, 'wide', [(i, i ^ 2) for i in range(wide)])  7.36 us
    all_to_all x1, waiting for transfers between devices, body(): out = lax.all_to_all(out, both, 0, 0, axis_index_groups=groups, tiled=True)  6.46 us
    all_to_all x1, starting transfers between devices, spread(): return lax.all_to_all(x, 'narrow', 0, 0, tiled=True)  5.83 us
    add x3, other arithmetic, body(): rows_of(grads, mine + starts[k], sizes[k])  5.01 us
  transfers between devices with their start and end apart: 16, of which 8 were waited for; matrix products, arithmetic and copies ran while one was open for 14% of the time, Pallas kernels for 27%

profile of v1, /device:TPU:0, one launch (start us, length us, event | category | flops | bytes accessed | tf_op | source)
XLA Modules:
  0.0 138.4 jit_solution(859400644258200349)
XLA Ops:
  0.7 1.5 %constant_dynamic-slice_fusion = (bf16[3,16,8192]{2,1,0:T(8,128)(2,1)S(1)}, bf16[3,16,8192]{2,1,0:T(8,128)(2,1)S(1)}) fusion(bf16[28,16,8192]{2,1,0:T(8,128)(2,1)} %bitcast.52, s32[]{:T(128)S(6)} %select_n.59, s32[]{:T(128)S(6)} %select_n.57), kind=kLoop, calls=%fused_computation.21 | loop fusion | bytes 3145736 | tf_op jit(solution)/shard_map/dynamic_slice | solution.py:282
  2.1 0.6 collective-permute-start
  2.7 1.9 %collective-permute-done = bf16[48,8192]{1,0:T(8,128)(2,1)S(1)} collective-permute-done((bf16[48,8192]{1,0:T(8,128)(2,1)S(1)}, bf16[48,8192]{1,0:T(8,128)(2,1)S(1)}, u32[]{:S(2)}, u32[]{:S(2)}) %collective-permute-start) | collective-permute-done | bytes 786464 | tf_op jit(solution)/shard_map/ppermute | solution.py:274
  4.6 0.4 collective-permute-start.1
  5.0 0.1 bitcast_add_fusion.refs_2_
  5.1 2.7 %collective-permute-start.5 = (bf16[48,8192]{1,0:T(8,128)(2,1)S(1)}, bf16[48,8192]{1,0:T(8,128)(2,1)S(1)}, u32[]{:S(2)}, u32[]{:S(2)}) collective-permute-start(bf16[48,8192]{1,0:T(8,128)(2,1)S(1)} %bitcast_add_fusion.refs_2_), channel_id=1, source_target_pairs={{0,16},{8,24},{16,0},{24,8},{1,17},{9,25},{17,1},{25,9},{2,18},{10... | collective-permute-start | bytes 2359304 | tf_op jit(solution)/shard_map/ppermute | solution.py:275
  7.8 0.7 convert_element_type.18
  8.5 0.8 select_reduce_fusion
  9.2 0.7 fusion.7
  10.0 0.7 broadcast_in_dim.4
  10.7 5.8 %all-to-all-start = ((bf16[8,2,3712]{2,1,0:T(2,128)(2,1)}), bf16[8,2,3712]{2,1,0:T(2,128)(2,1)S(1)}, u32[]{:S(2)}, u32[]{:S(2)}) async-start(bf16[8,2,3712]{2,1,0:T(2,128)(2,1)} %broadcast_in_dim.4), calls=%async_computation | async-start | bytes 237568 | tf_op jit(solution)/shard_map/all_to_all | solution.py:300
  16.5 9.4 %collective-permute-done.5.refs_3_ = bf16[48,8192]{1,0:T(8,128)(2,1)S(1)} collective-permute-done((bf16[48,8192]{1,0:T(8,128)(2,1)S(1)}, bf16[48,8192]{1,0:T(8,128)(2,1)S(1)}, u32[]{:S(2)}, u32[]{:S(2)}) %collective-permute-start.5) | collective-permute-done | bytes 786464 | tf_op jit(solution)/shard_map/ppermute | solution.py:275
  25.9 0.0 collective-permute-done.1.refs_1_
  25.9 1.9 %dynamic-slice_add_fusion = bf16[4,16,8192]{2,1,0:T(8,128)(2,1)S(1)} fusion(bf16[28,16,8192]{2,1,0:T(8,128)(2,1)} %bitcast.5, s32[]{:T(128)S(6)} %select_n.55, bf16[28,16,8192]{2,1,0:T(8,128)(2,1)} %bitcast.54), kind=kLoop, calls=%fused_computation.3 | loop fusion | flops 524288 | bytes 3145732 | tf_op jit(solution)/shard_map/add | solution.py:295
  27.9 0.1 copy.48
  28.0 0.2 collective-permute-start.8
  28.2 1.7 %collective-permute-start.6 = (bf16[64,8192]{1,0:T(8,128)(2,1)S(1)}, bf16[64,8192]{1,0:T(8,128)(2,1)}, u32[]{:S(2)}, u32[]{:S(2)}) collective-permute-start(bf16[64,8192]{1,0:T(8,128)(2,1)S(1)} %bitcast.44), channel_id=1, source_target_pairs={{0,16},{8,24},{16,0},{24,8},{1,17},{9,25},{17,1},{25,9},{2,18},{10... | collective-permute-start | bytes 3145736 | tf_op jit(solution)/shard_map/ppermute | solution.py:275
  30.0 9.0 %fusion.2 = f32[2,16,1024]{2,1,0:T(8,128)S(1)} fusion(bf16[3584,2,1024]{2,1,0:T(2,128)(2,1)} %param.12, bf16[16,3712]{1,0:T(8,128)(2,1)S(1)} %reshape.56), kind=kOutput, calls=%fused_computation.2 | convolution fusion | flops 234881024 | bytes 14925824 | tf_op jit(solution)/shard_map/td,dgu->gtu/dot_general | solution.py:221
  39.0 0.0 collective-permute-done.8
  39.0 0.1 convert_bitcast_fusion.refs_12_.refs_10_.refs_7_
  39.1 0.0 collective-permute-done.7.refs_2_
  39.1 4.6 %shard_map.111 = (bf16[448,8192]{1,0:T(8,128)(2,1)}, f32[448,8192]{1,0:T(8,128)}, f32[448,8192]{1,0:T(8,128)}, f32[8,128]{1,0:T(8,128)S(1)}) custom-call(s32[1]{0:T(128)} %bitcast.21.base, bf16[448,8192]{1,0:T(8,128)(2,1)} %bitcast.55, bf16[448,8192]{1,0:T(8,128)(2,1)} %collective-permute-done.1.refs_1_, bf16[48,8192]{1,0:T(8,128)(2,1)} %collective-permute-done.7.refs_2_, ...), custom_call_target="tpu_custom_call" | custom-call | flops 15728640 | bytes 10223616 | tf_op jit(solution)/shard_map/pallas_call | solution.py:181
  43.6 10.0 %collective-permute-done.6.refs_5_ = bf16[64,8192]{1,0:T(8,128)(2,1)} collective-permute-done((bf16[64,8192]{1,0:T(8,128)(2,1)S(1)}, bf16[64,8192]{1,0:T(8,128)(2,1)}, u32[]{:S(2)}, u32[]{:S(2)}) %collective-permute-start.6) | collective-permute-done | bytes 1048608 | tf_op jit(solution)/shard_map/ppermute | solution.py:275
  53.7 1.5 %dynamic-slice_add_fusion.1 = bf16[3,16,8192]{2,1,0:T(8,128)(2,1)S(1)} fusion(bf16[28,16,8192]{2,1,0:T(8,128)(2,1)} %bitcast.11, s32[]{:T(128)S(6)} %select_n.65, bf16[28,16,8192]{2,1,0:T(8,128)(2,1)} %bitcast.56), kind=kLoop, calls=%fused_computation.5 | loop fusion | flops 393216 | bytes 2359300 | tf_op jit(solution)/shard_map/add | solution.py:295
  55.1 1.8 %collective-permute-start.4 = (bf16[48,8192]{1,0:T(8,128)(2,1)S(1)}, bf16[48,8192]{1,0:T(8,128)(2,1)}, u32[]{:S(2)}, u32[]{:S(2)}) collective-permute-start(bf16[48,8192]{1,0:T(8,128)(2,1)S(1)} %bitcast.46), channel_id=1, source_target_pairs={{0,16},{8,24},{16,0},{24,8},{1,17},{9,25},{17,1},{25,9},{2,18},{10... | collective-permute-start | bytes 2359304 | tf_op jit(solution)/shard_map/ppermute | solution.py:275
  57.0 14.9 %all_to_all.15.refs_10_.refs_8_.refs_5_ = bf16[8,16,1024]{2,1,0:T(8,128)(2,1)S(1)} all-to-all(bf16[8,16,1024]{2,1,0:T(8,128)(2,1)S(1)} %broadcast_in_dim.5), channel_id=1, replica_groups=mesh['wide'=4,'narrow'=8] {'narrow'}, dimensions={0} | all-to-all | bytes 524288 | tf_op jit(solution)/shard_map/all_to_all | solution.py:300
  71.9 0.1 pad_add_fusion.1.base
  72.0 1.5 %collective-permute-done.10.refs_11_.refs_9_.refs_6_ = bf16[8,16,1024]{2,1,0:T(8,128)(2,1)S(1)} collective-permute-done((bf16[8,16,1024]{2,1,0:T(8,128)(2,1)S(1)}, bf16[8,16,1024]{2,1,0:T(8,128)(2,1)S(1)}, u32[]{:S(2)}, u32[]{:S(2)}) %collective-permute-start.10) | collective-permute-done | bytes 262176 | tf_op jit(solution)/shard_map/ppermute | solution.py:274
  73.4 1.1 copy-done.1
  74.6 13.5 %shard_map.112 = (bf16[448,8192]{1,0:T(8,128)(2,1)}, f32[448,8192]{1,0:T(8,128)}, f32[448,8192]{1,0:T(8,128)}, bf16[32,112]{1,0:T(8,128)(2,1)S(1)}, f32[8,128]{1,0:T(8,128)S(1)}) custom-call(s32[3]{0:T(128)S(1)} %pad_add_fusion.1.base, bf16[448,8192]{1,0:T(8,128)(2,1)} %bitcast.57, ...), custom_call_target="tpu_custom_call", output_to_operand_aliasing={{0}: (14, {}), {1}: (15, {}), {2}: (16, {})} | custom-call | flops 149946368 | bytes 37486592 | tf_op jit(solution)/shard_map/pallas_call | solution.py:181
  88.1 0.2 collective-permute-start.11
  88.3 1.6 %dynamic-slice_add_fusion.2 = (bf16[2,16,8192]{2,1,0:T(8,128)(2,1)S(1)}, bf16[2,16,8192]{2,1,0:T(8,128)(2,1)S(1)}) fusion(bf16[28,16,8192]{2,1,0:T(8,128)(2,1)} %bitcast.11, s32[]{:T(128)S(6)} %select_n.63, bf16[28,16,8192]{2,1,0:T(8,128)(2,1)} %bitcast.58, s32[]{:T(128)S(6)} %select_n.61), kind=kLoop, calls=%fused_computation.6 | loop fusion | flops 524288 | bytes 3145736 | tf_op jit(solution)/shard_map/add | solution.py:295
  89.9 0.6 collective-permute-start.3
  90.5 0.1 pad_add_fusion.base
  90.6 0.1 collective-permute-done.11.refs_4_
  90.7 8.4 %shard_map.113 = (bf16[448,8192]{1,0:T(8,128)(2,1)}, f32[448,8192]{1,0:T(8,128)}, f32[448,8192]{1,0:T(8,128)}, bf16[32,48]{1,0:T(8,128)(2,1)S(1)}, f32[8,128]{1,0:T(8,128)S(1)}) custom-call(s32[2]{0:T(128)S(1)} %pad_add_fusion.base, bf16[448,8192]{1,0:T(8,128)(2,1)} %bitcast.59, ...), custom_call_target="tpu_custom_call", output_to_operand_aliasing={{0}: (12, {}), {1}: (13, {}), {2}: (14, {})} | custom-call | flops 81788928 | bytes 20447232 | tf_op jit(solution)/shard_map/pallas_call | solution.py:181
  99.1 5.3 %collective-permute-done.3.refs_1_ = bf16[32,8192]{1,0:T(8,128)(2,1)} collective-permute-done((bf16[32,8192]{1,0:T(8,128)(2,1)S(1)}, bf16[32,8192]{1,0:T(8,128)(2,1)}, u32[]{:S(2)}, u32[]{:S(2)}) %collective-permute-start.3) | collective-permute-done | bytes 524320 | tf_op jit(solution)/shard_map/ppermute | solution.py:275
  104.3 0.5 collective-permute-start.2
  104.9 3.8 %shard_map.114 = (bf16[448,8192]{1,0:T(8,128)(2,1)}, f32[448,8192]{1,0:T(8,128)}, f32[448,8192]{1,0:T(8,128)}, bf16[32,32]{1,0:T(8,128)(2,1)S(1)}, f32[8,128]{1,0:T(8,128)S(1)}) custom-call(s32[1]{0:T(128)} %bitcast.23.base, bf16[32,8192]{1,0:T(8,128)(2,1)S(1)} %bitcast.51, ...), custom_call_target="tpu_custom_call", output_to_operand_aliasing={{0}: (9, {}), {1}: (10, {}), {2}: (11, {})} | custom-call | flops 27262976 | bytes 6815744 | tf_op jit(solution)/shard_map/pallas_call | solution.py:181
  108.6 3.7 %shard_map.115 = (bf16[448,8192]{1,0:T(8,128)(2,1)}, f32[448,8192]{1,0:T(8,128)}, f32[448,8192]{1,0:T(8,128)}, f32[8,128]{1,0:T(8,128)S(1)}) custom-call(s32[1]{0:T(128)} %bitcast.13.base, bf16[448,8192]{1,0:T(8,128)(2,1)} %bitcast.60, bf16[448,8192]{1,0:T(8,128)(2,1)} %collective-permute-done.1.refs_1_, ...), custom_call_target="tpu_custom_call", output_to_operand_aliasing={{0}: (7, {}), {1}: (8, {}), {2}: (9, {})} | custom-call | flops 10485760 | bytes 6815744 | tf_op jit(solution)/shard_map/pallas_call | solution.py:181
  112.4 6.3 %collective-permute-done.2.refs_1_ = bf16[32,8192]{1,0:T(8,128)(2,1)S(1)} collective-permute-done((bf16[32,8192]{1,0:T(8,128)(2,1)S(1)}, bf16[32,8192]{1,0:T(8,128)(2,1)S(1)}, u32[]{:S(2)}, u32[]{:S(2)}) %collective-permute-start.2) | collective-permute-done | bytes 524320 | tf_op jit(solution)/shard_map/ppermute | solution.py:275
  118.7 3.7 %shard_map.116 = (bf16[448,8192]{1,0:T(8,128)(2,1)}, f32[448,8192]{1,0:T(8,128)}, f32[448,8192]{1,0:T(8,128)}, bf16[32,32]{1,0:T(8,128)(2,1)S(1)}, f32[8,128]{1,0:T(8,128)S(1)}) custom-call(s32[1]{0:T(128)} %bitcast.24.base, bf16[32,8192]{1,0:T(8,128)(2,1)S(1)} %bitcast.49, ...), custom_call_target="tpu_custom_call", output_to_operand_aliasing={{0}: (9, {}), {1}: (10, {}), {2}: (11, {})} | custom-call | flops 27262976 | bytes 6815744 | tf_op jit(solution)/shard_map/pallas_call | solution.py:181
  122.4 0.1 pad_maximum_fusion
  122.5 0.6 broadcast_select_fusion
  123.1 3.8 %all-to-all-start.2 = ((bf16[16,2,224]{2,1,0:T(2,128)(2,1)}), bf16[16,2,224]{2,1,0:T(2,128)(2,1)S(1)}, u32[]{:S(2)}, u32[]{:S(2)}) async-start(bf16[16,2,224]{2,1,0:T(2,128)(2,1)} %bitcast.25), calls=%async_computation.2 | async-start | bytes 32768 | tf_op jit(solution)/shard_map/all_to_all | solution.py:353
  126.9 6.5 %all-to-all-done.2 = bf16[16,2,224]{2,1,0:T(2,128)(2,1)S(1)} async-done(((bf16[16,2,224]{2,1,0:T(2,128)(2,1)}), bf16[16,2,224]{2,1,0:T(2,128)(2,1)S(1)}, u32[]{:S(2)}, u32[]{:S(2)}) %all-to-all-start.2) | async-done | bytes 14368 | tf_op jit(solution)/shard_map/all_to_all | solution.py:353
  133.4 0.7 reshape.61
  134.1 4.3 %shard_map.117 = (bf16[448,8192]{1,0:T(8,128)(2,1)}, f32[448,8192]{1,0:T(8,128)}, f32[448,8192]{1,0:T(8,128)}, f32[8,128]{1,0:T(8,128)}) custom-call(s32[1]{0:T(128)} %bitcast.base, bf16[448,8192]{1,0:T(8,128)(2,1)} %bitcast.61, bf16[448,8192]{1,0:T(8,128)(2,1)} %collective-permute-done.1.refs_1_, ...), custom_call_target="tpu_custom_call", output_to_operand_aliasing={{0}: (7, {}), {1}: (8, {}), {2}: (9, {})} | custom-call | flops 10485760 | bytes 6815744 | tf_op jit(solution)/shard_map/pallas_call | solution.py:181
  (20 shorter events, 0.2 us)
Async XLA Ops:
  2.1 2.5 %collective-permute-start = (bf16[48,8192]{1,0:T(8,128)(2,1)S(1)}, bf16[48,8192]{1,0:T(8,128)(2,1)S(1)}, u32[]{:S(2)}, u32[]{:S(2)}) collective-permute-start(bf16[48,8192]{1,0:T(8,128)(2,1)S(1)} %bitcast.62), channel_id=1, source_target_pairs={{0,8},{8,0},{16,24},{24,16},{1,9},{9,1},{17,25},{25,17},{2,10},{10... | collective-permute-start | bytes 2359304 | tf_op jit(solution)/shard_map/ppermute | solution.py:274
  4.6 21.3 %collective-permute-start.1 = (bf16[448,8192]{1,0:T(8,128)(2,1)}, bf16[448,8192]{1,0:T(8,128)(2,1)}, u32[]{:S(2)}, u32[]{:S(2)}) collective-permute-start(bf16[448,8192]{1,0:T(8,128)(2,1)} %bitcast.53), channel_id=1, source_target_pairs={{0,8},{8,0},{16,24},{24,16},{1,9},{9,1},{17,25},{25,17},{2,10},{10... | collective-permute-start | bytes 22020104 | tf_op jit(solution)/shard_map/ppermute | solution.py:274
  5.1 20.8 %collective-permute-start.5 = (bf16[48,8192]{1,0:T(8,128)(2,1)S(1)}, bf16[48,8192]{1,0:T(8,128)(2,1)S(1)}, u32[]{:S(2)}, u32[]{:S(2)}) collective-permute-start(bf16[48,8192]{1,0:T(8,128)(2,1)S(1)} %bitcast_add_fusion.refs_2_), channel_id=1, source_target_pairs={{0,16},{8,24},{16,0},{24,8},{1,17},{9,25},{17,1},{25,9},{2,18},{10... | collective-permute-start | bytes 2359304 | tf_op jit(solution)/shard_map/ppermute | solution.py:275
  10.7 17.2 %all-to-all-start = ((bf16[8,2,3712]{2,1,0:T(2,128)(2,1)}), bf16[8,2,3712]{2,1,0:T(2,128)(2,1)S(1)}, u32[]{:S(2)}, u32[]{:S(2)}) async-start(bf16[8,2,3712]{2,1,0:T(2,128)(2,1)} %broadcast_in_dim.4), calls=%async_computation | async-start | bytes 237568 | tf_op jit(solution)/shard_map/all_to_all | solution.py:300
  25.9 17.7 %copy-start = (bf16[48,8192]{1,0:T(8,128)(2,1)}, bf16[48,8192]{1,0:T(8,128)(2,1)S(1)}, u32[]{:S(2)}) copy-start(bf16[48,8192]{1,0:T(8,128)(2,1)S(1)} %collective-permute-done.5.refs_3_) | copy-start | bytes 2359300
  25.9 13.2 %collective-permute-start.7 = (bf16[48,8192]{1,0:T(8,128)(2,1)S(1)}, bf16[48,8192]{1,0:T(8,128)(2,1)}, u32[]{:S(2)}, u32[]{:S(2)}) collective-permute-start(bf16[48,8192]{1,0:T(8,128)(2,1)S(1)} %collective-permute-done.5.refs_3_), channel_id=1, source_target_pairs={{0,8},{8,0},{16,24},{24,16},{1,9},{9,1},{17,25},{25,17},{2,10},{10... | collective-permute-start | bytes 2359304 | tf_op jit(solution)/shard_map/ppermute | solution.py:274
  28.0 11.0 %collective-permute-start.8 = (bf16[16,8]{0,1:T(8,128)(2,1)S(1)}, bf16[16,8]{0,1:T(8,128)(2,1)S(1)}, u32[]{:S(2)}, u32[]{:S(2)}) collective-permute-start(bf16[16,8]{0,1:T(8,128)(2,1)S(1)} %copy.48), channel_id=1, source_target_pairs={{0,8},{8,0},{16,24},{24,16},{1,9},{9,1},{17,25},{25,17},{2,10},{10... | collective-permute-start | bytes 776 | tf_op jit(solution)/shard_map/ppermute | solution.py:274
  28.2 25.5 %collective-permute-start.6 = (bf16[64,8192]{1,0:T(8,128)(2,1)S(1)}, bf16[64,8192]{1,0:T(8,128)(2,1)}, u32[]{:S(2)}, u32[]{:S(2)}) collective-permute-start(bf16[64,8192]{1,0:T(8,128)(2,1)S(1)} %bitcast.44), channel_id=1, source_target_pairs={{0,16},{8,24},{16,0},{24,8},{1,17},{9,25},{17,1},{25,9},{2,18},{10... | collective-permute-start | bytes 3145736 | tf_op jit(solution)/shard_map/ppermute | solution.py:275
  53.7 19.8 %collective-permute-start.9 = (bf16[64,8192]{1,0:T(8,128)(2,1)}, bf16[64,8192]{1,0:T(8,128)(2,1)}, u32[]{:S(2)}, u32[]{:S(2)}) collective-permute-start(bf16[64,8192]{1,0:T(8,128)(2,1)} %collective-permute-done.6.refs_5_), channel_id=1, source_target_pairs={{0,8},{8,0},{16,24},{24,16},{1,9},{9,1},{17,25},{25,17},{2,10},{10... | collective-permute-start | bytes 3145736 | tf_op jit(solution)/shard_map/ppermute | solution.py:274
  55.1 33.0 %collective-permute-start.4 = (bf16[48,8192]{1,0:T(8,128)(2,1)S(1)}, bf16[48,8192]{1,0:T(8,128)(2,1)}, u32[]{:S(2)}, u32[]{:S(2)}) collective-permute-start(bf16[48,8192]{1,0:T(8,128)(2,1)S(1)} %bitcast.46), channel_id=1, source_target_pairs={{0,16},{8,24},{16,0},{24,8},{1,17},{9,25},{17,1},{25,9},{2,18},{10... | collective-permute-start | bytes 2359304 | tf_op jit(solution)/shard_map/ppermute | solution.py:275
  71.9 1.5 %collective-permute-start.10 = (bf16[8,16,1024]{2,1,0:T(8,128)(2,1)S(1)}, bf16[8,16,1024]{2,1,0:T(8,128)(2,1)S(1)}, u32[]{:S(2)}, u32[]{:S(2)}) collective-permute-start(bf16[8,16,1024]{2,1,0:T(8,128)(2,1)S(1)} %all_to_all.15.refs_10_.refs_8_.refs_5_), channel_id=1, source_target_pairs={{0,8},{8,0},{16,24},{24,16},{1,9},{9,1},{17,25},{25,17},{2,10},{10... | collective-permute-start | bytes 786440 | tf_op jit(solution)/shard_map/ppermute | solution.py:274
  73.4 1.1 copy-start.1
  88.1 2.6 %collective-permute-start.11 = (bf16[48,8192]{1,0:T(8,128)(2,1)}, bf16[48,8192]{1,0:T(8,128)(2,1)S(1)}, u32[]{:S(2)}, u32[]{:S(2)}) collective-permute-start(bf16[48,8192]{1,0:T(8,128)(2,1)} %collective-permute-done.4.refs_3_), channel_id=1, source_target_pairs={{0,8},{8,0},{16,24},{24,16},{1,9},{9,1},{17,25},{25,17},{2,10},{10... | collective-permute-start | bytes 2359304 | tf_op jit(solution)/shard_map/ppermute | solution.py:274
  89.9 14.4 %collective-permute-start.3 = (bf16[32,8192]{1,0:T(8,128)(2,1)S(1)}, bf16[32,8192]{1,0:T(8,128)(2,1)}, u32[]{:S(2)}, u32[]{:S(2)}) collective-permute-start(bf16[32,8192]{1,0:T(8,128)(2,1)S(1)} %bitcast.50), channel_id=1, source_target_pairs={{0,16},{8,24},{16,0},{24,8},{1,17},{9,25},{17,1},{25,9},{2,18},{10... | collective-permute-start | bytes 1572872 | tf_op jit(solution)/shard_map/ppermute | solution.py:275
  104.3 4.3 %collective-permute-start.12 = (bf16[32,8192]{1,0:T(8,128)(2,1)}, bf16[32,8192]{1,0:T(8,128)(2,1)S(1)}, u32[]{:S(2)}, u32[]{:S(2)}) collective-permute-start(bf16[32,8192]{1,0:T(8,128)(2,1)} %collective-permute-done.3.refs_1_), channel_id=1, source_target_pairs={{0,8},{8,0},{16,24},{24,16},{1,9},{9,1},{17,25},{25,17},{2,10},{10... | collective-permute-start | bytes 1572872 | tf_op jit(solution)/shard_map/ppermute | solution.py:274
  104.3 14.3 %collective-permute-start.2 = (bf16[32,8192]{1,0:T(8,128)(2,1)S(1)}, bf16[32,8192]{1,0:T(8,128)(2,1)S(1)}, u32[]{:S(2)}, u32[]{:S(2)}) collective-permute-start(bf16[32,8192]{1,0:T(8,128)(2,1)S(1)} %bitcast.48), channel_id=1, source_target_pairs={{0,16},{8,24},{16,0},{24,8},{1,17},{9,25},{17,1},{25,9},{2,18},{10... | collective-permute-start | bytes 1572872 | tf_op jit(solution)/shard_map/ppermute | solution.py:275
  118.7 15.4 %collective-permute-start.13 = (bf16[32,8192]{1,0:T(8,128)(2,1)S(1)}, bf16[32,8192]{1,0:T(8,128)(2,1)S(1)}, u32[]{:S(2)}, u32[]{:S(2)}) collective-permute-start(bf16[32,8192]{1,0:T(8,128)(2,1)S(1)} %collective-permute-done.2.refs_1_), channel_id=1, source_target_pairs={{0,8},{8,0},{16,24},{24,16},{1,9},{9,1},{17,25},{25,17},{2,10},{10... | collective-permute-start | bytes 1572872 | tf_op jit(solution)/shard_map/ppermute | solution.py:274
  123.1 10.3 %all-to-all-start.2 = ((bf16[16,2,224]{2,1,0:T(2,128)(2,1)}), bf16[16,2,224]{2,1,0:T(2,128)(2,1)S(1)}, u32[]{:S(2)}, u32[]{:S(2)}) async-start(bf16[16,2,224]{2,1,0:T(2,128)(2,1)} %bitcast.25), calls=%async_computation.2 | async-start | bytes 32768 | tf_op jit(solution)/shard_map/all_to_all | solution.py:353
